TPU v7x, 128 devices: a whole 4x4x4 slice. The times are simulated.
128 devices in a mesh: freq: 8 (over x, z_hi), blk: 16 (over y, z_lo, core).
Axes of the slice: x: 4, y: 4, z: 4 (z_hi: 2, z_lo: 2; z = z_hi * 2 + z_lo), core: 2. Of those that a mesh axis runs over, the one named last changes fastest.
Arguments:
- reflection: bfloat16 [16, 2, 6144, 6144], P('freq', None, 'blk'), as said below
- direct_focus: bfloat16 [32, 1024, 6144], P('freq', None, 'blk'), may hold values from -6 to 6
- onset: int32 [32, 6144], P('freq', 'blk'), may hold values from 64 to 81
Outputs:
- focused: bfloat16 [32, 1024, 6144], P('freq', None, 'blk')
Inputs may be any that keep to these rules, and one draw needn't show every extreme that they name: For every frequency, the real and the imaginary matrix of reflection are each symmetric (source-receiver reciprocity).
All inputs are finite; a program needn't handle non-finite values.
Results may differ from a plain program's by a relative error of at most 0.02.
Values may be sent and summed in bfloat16 or wider, within the bound.
No kernel may reach another device: no remote copies, remote signals or barrier semaphores. Data moves between devices by JAX's collectives and lax.ppermute only.
A program may use at most 128 MiB of HBM per device.

v0:
```python
import math

import jax
import jax.numpy as jnp
from jax import lax
from jax.sharding import PartitionSpec as P

ITERS = 3


def make_tables(count_time, count_freq):
    moments = jnp.arange(count_time, dtype=jnp.int32)
    frequency_bins = 1 + jnp.arange(count_freq, dtype=jnp.int32) * (count_time // (2 * count_freq))
    phase = (frequency_bins[:, None] * moments[None, :] % count_time).astype(jnp.float32) * (
        2.0 * math.pi / count_time
    )
    cosine = jnp.cos(phase)
    sine_part = jnp.sin(phase)
    stacked = jnp.concatenate([cosine, -sine_part], 0)
    forward_table = (stacked * count_time ** (-0.5)).astype(jnp.bfloat16)
    inverse_table = (stacked.T * math.sqrt(2.0 / count_freq)).astype(jnp.bfloat16)
    return (forward_table, inverse_table)


def shards(reflection, direct_focus, onset):
    local_freq = reflection.shape[0]
    all_freq = local_freq * lax.axis_size("freq")
    focal_local, count_time, rows = direct_focus.shape
    forward_table, inverse_table = make_tables(count_time, all_freq)
    moments = jnp.arange(count_time, dtype=jnp.int32)
    signed_time = jnp.where(moments < count_time // 2, moments, moments - count_time)
    window = jnp.abs(signed_time)[None, :, None] < onset[:, None, :]

    def to_spectrum(field):
        spectrum = jnp.einsum(
            "kt,ftr->fkr", forward_table, field, preferred_element_type=jnp.float32
        )
        spectrum = spectrum.reshape(focal_local, 2, all_freq, rows).astype(jnp.bfloat16)
        return lax.all_to_all(spectrum, "freq", split_axis=2, concat_axis=0, tiled=True)

    def to_time(values):
        gathered = lax.all_to_all(values, "freq", split_axis=0, concat_axis=2, tiled=True)
        flat = gathered.reshape(focal_local, 2 * all_freq, rows)
        return jnp.einsum("tk,fkr->ftr", inverse_table, flat, preferred_element_type=jnp.float32)

    def apply_reflection(spectrum, orient):
        parts = jnp.einsum(
            "jars,fbjs->fabjr",
            reflection,
            lax.all_gather(spectrum, "blk", axis=3, tiled=True),
            preferred_element_type=jnp.float32,
        )
        real_part = parts[:, 0, 0] - orient * parts[:, 1, 1]
        imag_part = parts[:, 0, 1] + orient * parts[:, 1, 0]
        summed = jnp.stack([real_part, imag_part], 1)
        return summed.astype(jnp.bfloat16)

    focus = direct_focus
    for repeat in range(ITERS):
        values = apply_reflection(to_spectrum(focus), 1.0)
        upgoing = jnp.where(window, to_time(values), 0.0).astype(jnp.bfloat16)
        values = apply_reflection(to_spectrum(upgoing), -1.0)
        focus = (direct_focus.astype(jnp.float32) - jnp.where(window, to_time(values), 0.0)).astype(
            jnp.bfloat16
        )
    return focus


def solution(mesh):
    return jax.shard_map(
        shards,
        mesh=mesh,
        in_specs=(P("freq", None, "blk", None), P("freq", None, "blk"), P("freq", "blk")),
        out_specs=P("freq", None, "blk"),
        check_vma=False,
    )
```

profile of v0, /device:TPU:0, one launch (start us, length us, event | category | flops | bytes accessed | tf_op | source)
XLA Modules:
  0.0 439.5 jit_solution(6814414630698046546)
XLA Ops:
  9.6 15.3 %all_to_all.198 = bf16[4,2,16,384]{3,1,0,2:T(2,128)(2,1)S(1)} all-to-all(bf16[4,2,16,384]{3,1,0,2:T(2,128)(2,1)S(1)} %copy.60), channel_id=1, replica_groups=mesh['freq'=8,'blk'=16] {'freq'}, dimensions={2} | all-to-all | bytes 196608 | tf_op jit(solution)/shard_map/all_to_all | solution.py:39
  25.7 31.3 %all-gather.7.cloned.1.call-done = bf16[32,2,2,6144]{3,0,1,2:T(8,128)(2,1)} async-done(((bf16[32,2,2,384]{3,0,1,2:T(8,128)(2,1)}), bf16[32,2,2,6144]{3,0,1,2:T(8,128)(2,1)}) %all-gather.7.cloned.1.call-update) | async-done | bytes 1572880 | tf_op jit(solution)/shard_map/all_gather | solution.py:50
  56.9 10.2 %fusion.63 = f32[32,2,2,2,384]{4,0,1,2,3:T(8,128)S(1)} fusion(bf16[2,2,384,6144]{3,2,1,0:T(8,128)(2,1)} %param.3, bf16[32,2,2,6144]{3,0,1,2:T(8,128)(2,1)} %all-gather.7.cloned.1.call-done), kind=kOutput, calls=%fused_computation.54 | convolution fusion | flops 1207959552 | bytes 20840448 | tf_op jit(solution)/shard_map/jars,fbjs->fabjr/dot_general | solution.py:47
  67.9 6.4 %all-to-all-start.1 = ((bf16[32,2,2,384]{3,2,1,0:T(2,128)(2,1)}), bf16[32,2,2,384]{3,2,1,0:T(2,128)(2,1)S(1)}, u32[]{:S(2)}, u32[]{:S(2)}) async-start(bf16[32,2,2,384]{3,2,1,0:T(2,128)(2,1)} %copy.64), calls=%async_computation.1 | async-start | bytes 196608 | tf_op jit(solution)/shard_map/all_to_all | solution.py:42
  74.4 7.8 %all-to-all-done.1 = bf16[32,2,2,384]{3,2,1,0:T(2,128)(2,1)S(1)} async-done(((bf16[32,2,2,384]{3,2,1,0:T(2,128)(2,1)}), bf16[32,2,2,384]{3,2,1,0:T(2,128)(2,1)S(1)}, u32[]{:S(2)}, u32[]{:S(2)}) %all-to-all-start.1) | async-done | bytes 98336 | tf_op jit(solution)/shard_map/all_to_all | solution.py:42
  84.2 10.4 %all_to_all.199 = bf16[4,2,16,384]{3,1,0,2:T(2,128)(2,1)S(1)} all-to-all(bf16[4,2,16,384]{3,1,0,2:T(2,128)(2,1)S(1)} %copy.68), channel_id=1, replica_groups=mesh['freq'=8,'blk'=16] {'freq'}, dimensions={2} | all-to-all | bytes 196608 | tf_op jit(solution)/shard_map/all_to_all | solution.py:39
  95.4 29.9 %all-gather.9.cloned.1.call-done = bf16[32,2,2,6144]{3,0,1,2:T(8,128)(2,1)} async-done(((bf16[32,2,2,384]{3,0,1,2:T(8,128)(2,1)}), bf16[32,2,2,6144]{3,0,1,2:T(8,128)(2,1)}) %all-gather.9.cloned.1.call-update) | async-done | bytes 1572880 | tf_op jit(solution)/shard_map/all_gather | solution.py:50
  125.3 10.2 %fusion.68 = f32[32,2,2,2,384]{4,0,1,2,3:T(8,128)S(1)} fusion(bf16[2,2,384,6144]{3,2,1,0:T(8,128)(2,1)} %param.3, bf16[32,2,2,6144]{3,0,1,2:T(8,128)(2,1)} %all-gather.9.cloned.1.call-done), kind=kOutput, calls=%fused_computation.55 | convolution fusion | flops 1207959552 | bytes 20840448 | tf_op jit(solution)/shard_map/jars,fbjs->fabjr/dot_general | solution.py:47
  136.4 6.4 %all-to-all-start.3 = ((bf16[32,2,2,384]{3,2,1,0:T(2,128)(2,1)}), bf16[32,2,2,384]{3,2,1,0:T(2,128)(2,1)S(1)}, u32[]{:S(2)}, u32[]{:S(2)}) async-start(bf16[32,2,2,384]{3,2,1,0:T(2,128)(2,1)} %copy.73), calls=%async_computation.3 | async-start | bytes 196608 | tf_op jit(solution)/shard_map/all_to_all | solution.py:42
  142.8 2.9 copy.59
  145.7 4.9 %all-to-all-done.3 = bf16[32,2,2,384]{3,2,1,0:T(2,128)(2,1)S(1)} async-done(((bf16[32,2,2,384]{3,2,1,0:T(2,128)(2,1)}), bf16[32,2,2,384]{3,2,1,0:T(2,128)(2,1)S(1)}, u32[]{:S(2)}, u32[]{:S(2)}) %all-to-all-start.3) | async-done | bytes 98336 | tf_op jit(solution)/shard_map/all_to_all | solution.py:42
  150.6 3.8 fusion.92
  154.6 10.4 %all_to_all.200 = bf16[4,2,16,384]{3,1,0,2:T(2,128)(2,1)S(1)} all-to-all(bf16[4,2,16,384]{3,1,0,2:T(2,128)(2,1)S(1)} %copy.77), channel_id=1, replica_groups=mesh['freq'=8,'blk'=16] {'freq'}, dimensions={2} | all-to-all | bytes 196608 | tf_op jit(solution)/shard_map/all_to_all | solution.py:39
  166.0 29.7 %all-gather.11.cloned.1.call-done = bf16[32,2,2,6144]{3,0,1,2:T(8,128)(2,1)} async-done(((bf16[32,2,2,384]{3,0,1,2:T(8,128)(2,1)}), bf16[32,2,2,6144]{3,0,1,2:T(8,128)(2,1)}) %all-gather.11.cloned.1.call-update) | async-done | bytes 1572880 | tf_op jit(solution)/shard_map/all_gather | solution.py:50
  195.7 10.2 %fusion.73 = f32[32,2,2,2,384]{4,0,1,2,3:T(8,128)S(1)} fusion(bf16[2,2,384,6144]{3,2,1,0:T(8,128)(2,1)} %param.3, bf16[32,2,2,6144]{3,0,1,2:T(8,128)(2,1)} %all-gather.11.cloned.1.call-done), kind=kOutput, calls=%fused_computation.56 | convolution fusion | flops 1207959552 | bytes 20840448 | tf_op jit(solution)/shard_map/jars,fbjs->fabjr/dot_general | solution.py:47
  206.1 14.0 %all_to_all.201 = bf16[32,2,2,384]{3,2,1,0:T(2,128)(2,1)S(1)} all-to-all(bf16[32,2,2,384]{3,2,1,0:T(2,128)(2,1)S(1)} %copy.81), channel_id=1, replica_groups=mesh['freq'=8,'blk'=16] {'freq'}, dimensions={0} | all-to-all | bytes 196608 | tf_op jit(solution)/shard_map/all_to_all | solution.py:42
  222.1 10.4 %all_to_all.202 = bf16[4,2,16,384]{3,1,0,2:T(2,128)(2,1)S(1)} all-to-all(bf16[4,2,16,384]{3,1,0,2:T(2,128)(2,1)S(1)} %copy.85), channel_id=1, replica_groups=mesh['freq'=8,'blk'=16] {'freq'}, dimensions={2} | all-to-all | bytes 196608 | tf_op jit(solution)/shard_map/all_to_all | solution.py:39
  233.4 29.9 %all-gather.13.cloned.1.call-done = bf16[32,2,2,6144]{3,0,1,2:T(8,128)(2,1)} async-done(((bf16[32,2,2,384]{3,0,1,2:T(8,128)(2,1)}), bf16[32,2,2,6144]{3,0,1,2:T(8,128)(2,1)}) %all-gather.13.cloned.1.call-update) | async-done | bytes 1572880 | tf_op jit(solution)/shard_map/all_gather | solution.py:50
  263.2 10.2 %fusion.53 = f32[32,2,2,2,384]{4,0,3,2,1:T(8,128)S(1)} fusion(bf16[2,2,384,6144]{3,2,1,0:T(8,128)(2,1)} %param.3, bf16[32,2,2,6144]{3,0,1,2:T(8,128)(2,1)} %all-gather.13.cloned.1.call-done), kind=kOutput, calls=%fused_computation.52 | convolution fusion | flops 1207959552 | bytes 20840448 | tf_op jit(solution)/shard_map/jars,fbjs->fabjr/dot_general | solution.py:47
  273.6 14.0 %all_to_all.203 = bf16[32,2,2,384]{3,2,1,0:T(2,128)(2,1)S(1)} all-to-all(bf16[32,2,2,384]{3,2,1,0:T(2,128)(2,1)S(1)} %copy.88), channel_id=1, replica_groups=mesh['freq'=8,'blk'=16] {'freq'}, dimensions={0} | all-to-all | bytes 196608 | tf_op jit(solution)/shard_map/all_to_all | solution.py:42
  287.7 2.8 fusion.95
  290.6 10.4 %all_to_all.204 = bf16[4,2,16,384]{3,1,0,2:T(2,128)(2,1)S(1)} all-to-all(bf16[4,2,16,384]{3,1,0,2:T(2,128)(2,1)S(1)} %copy.92), channel_id=1, replica_groups=mesh['freq'=8,'blk'=16] {'freq'}, dimensions={2} | all-to-all | bytes 196608 | tf_op jit(solution)/shard_map/all_to_all | solution.py:39
  301.8 29.9 %all-gather.15.cloned.1.call-done = bf16[32,2,2,6144]{3,0,1,2:T(8,128)(2,1)} async-done(((bf16[32,2,2,384]{3,0,1,2:T(8,128)(2,1)}), bf16[32,2,2,6144]{3,0,1,2:T(8,128)(2,1)}) %all-gather.15.cloned.1.call-update) | async-done | bytes 1572880 | tf_op jit(solution)/shard_map/all_gather | solution.py:50
  331.7 10.2 %fusion.78 = f32[32,2,2,2,384]{4,0,1,2,3:T(8,128)S(1)} fusion(bf16[2,2,384,6144]{3,2,1,0:T(8,128)(2,1)} %param.3, bf16[32,2,2,6144]{3,0,1,2:T(8,128)(2,1)} %all-gather.15.cloned.1.call-done), kind=kOutput, calls=%fused_computation.57 | convolution fusion | flops 1207959552 | bytes 20840448 | tf_op jit(solution)/shard_map/jars,fbjs->fabjr/dot_general | solution.py:47
  342.1 14.0 %all_to_all.205 = bf16[32,2,2,384]{3,2,1,0:T(2,128)(2,1)S(1)} all-to-all(bf16[32,2,2,384]{3,2,1,0:T(2,128)(2,1)S(1)} %copy.96), channel_id=1, replica_groups=mesh['freq'=8,'blk'=16] {'freq'}, dimensions={0} | all-to-all | bytes 196608 | tf_op jit(solution)/shard_map/all_to_all | solution.py:42
  356.2 2.7 fusion.89
  359.0 10.4 %all_to_all.206 = bf16[4,2,16,384]{3,1,0,2:T(2,128)(2,1)S(1)} all-to-all(bf16[4,2,16,384]{3,1,0,2:T(2,128)(2,1)S(1)} %copy.100), channel_id=1, replica_groups=mesh['freq'=8,'blk'=16] {'freq'}, dimensions={2} | all-to-all | bytes 196608 | tf_op jit(solution)/shard_map/all_to_all | solution.py:39
  370.2 29.9 %all-gather.17.cloned.1.call-done = bf16[32,2,2,6144]{3,0,1,2:T(8,128)(2,1)} async-done(((bf16[32,2,2,384]{3,0,1,2:T(8,128)(2,1)}), bf16[32,2,2,6144]{3,0,1,2:T(8,128)(2,1)}) %all-gather.17.cloned.1.call-update) | async-done | bytes 1572880 | tf_op jit(solution)/shard_map/all_gather | solution.py:50
  400.1 10.2 %fusion.58 = f32[32,2,2,2,384]{4,0,3,2,1:T(8,128)S(1)} fusion(bf16[2,2,384,6144]{3,2,1,0:T(8,128)(2,1)} %param.3, bf16[32,2,2,6144]{3,0,1,2:T(8,128)(2,1)} %all-gather.17.cloned.1.call-done), kind=kOutput, calls=%fused_computation.53 | convolution fusion | flops 1207959552 | bytes 20840448 | tf_op jit(solution)/shard_map/jars,fbjs->fabjr/dot_general | solution.py:47
  410.5 14.0 %all_to_all.207 = bf16[32,2,2,384]{3,2,1,0:T(2,128)(2,1)S(1)} all-to-all(bf16[32,2,2,384]{3,2,1,0:T(2,128)(2,1)S(1)} %copy.103), channel_id=1, replica_groups=mesh['freq'=8,'blk'=16] {'freq'}, dimensions={0} | all-to-all | bytes 196608 | tf_op jit(solution)/shard_map/all_to_all | solution.py:42
  424.6 3.4 fusion.14
  428.0 4.6 %copy.105 = bf16[4,1024,384]{2,1,0:T(8,128)(2,1)} copy(bf16[4,1024,384]{1,2,0:T(8,128)(2,1)} %fusion.14) | data formatting | bytes 6291456 | tf_op jit(solution)/shard_map/convert_element_type | solution.py:63
  (80 shorter events, 14.3 us)
Async XLA Ops:
  6.5 50.4 %all-gather.7.cloned.1.call-start = ((), (), s32[]{:S(2)}) async-start(), calls=%async_computation.12 | async-start | bytes 1671168 | tf_op jit(solution)/shard_map/all_gather | solution.py:50
  6.9 75.3 %copy-start.2 = (bf16[32,1024,1]{1,0,2:T(8,128)(2,1)}, bf16[32,1024,1]{1,0,2:T(8,128)(2,1)S(1)}, u32[]{:S(2)}) copy-start(bf16[32,1024,1]{1,0,2:T(8,128)(2,1)S(1)} %get-tuple-element.10) | copy-start | bytes 196612
  6.9 75.3 %copy-start.4 = (bf16[32,1024,1]{1,0,2:T(8,128)(2,1)}, bf16[32,1024,1]{1,0,2:T(8,128)(2,1)S(1)}, u32[]{:S(2)}) copy-start(bf16[32,1024,1]{1,0,2:T(8,128)(2,1)S(1)} %get-tuple-element.9) | copy-start | bytes 196612
  25.6 56.6 %copy-start.6 = (s32[4,384]{1,0:T(4,128)S(1)}, s32[4,384]{1,0:T(4,128)}, u32[]{:S(2)}) copy-start(s32[4,384]{1,0:T(4,128)} %param.5) | copy-start | bytes 18436
  67.9 14.2 %all-to-all-start.1 = ((bf16[32,2,2,384]{3,2,1,0:T(2,128)(2,1)}), bf16[32,2,2,384]{3,2,1,0:T(2,128)(2,1)S(1)}, u32[]{:S(2)}, u32[]{:S(2)}) async-start(bf16[32,2,2,384]{3,2,1,0:T(2,128)(2,1)} %copy.64), calls=%async_computation.1 | async-start | bytes 196608 | tf_op jit(solution)/shard_map/all_to_all | solution.py:42
  74.4 51.0 %all-gather.9.cloned.1.call-start = ((), (), s32[]{:S(2)}) async-start(), calls=%async_computation.13 | async-start | bytes 1671168 | tf_op jit(solution)/shard_map/all_gather | solution.py:50
  95.4 47.4 %copy-start = (bf16[4,1024,384]{2,1,0:T(8,128)(2,1)S(1)}, bf16[4,1024,384]{2,1,0:T(8,128)(2,1)}, u32[]{:S(2)}) copy-start(bf16[4,1024,384]{2,1,0:T(8,128)(2,1)} %param.4) | copy-start | bytes 9437188
  135.6 15.0 %copy-start.3 = (bf16[32,1024,1]{1,0,2:T(8,128)(2,1)S(1)}, bf16[32,1024,1]{1,0,2:T(8,128)(2,1)}, u32[]{:S(2)}) copy-start(bf16[32,1024,1]{1,0,2:T(8,128)(2,1)} %copy-done.2) | copy-start | bytes 196612
  135.6 15.0 %copy-start.5 = (bf16[32,1024,1]{1,0,2:T(8,128)(2,1)S(1)}, bf16[32,1024,1]{1,0,2:T(8,128)(2,1)}, u32[]{:S(2)}) copy-start(bf16[32,1024,1]{1,0,2:T(8,128)(2,1)} %copy-done.4) | copy-start | bytes 196612
  136.4 14.2 %all-to-all-start.3 = ((bf16[32,2,2,384]{3,2,1,0:T(2,128)(2,1)}), bf16[32,2,2,384]{3,2,1,0:T(2,128)(2,1)S(1)}, u32[]{:S(2)}, u32[]{:S(2)}) async-start(bf16[32,2,2,384]{3,2,1,0:T(2,128)(2,1)} %copy.73), calls=%async_computation.3 | async-start | bytes 196608 | tf_op jit(solution)/shard_map/all_to_all | solution.py:42
  142.8 52.9 %all-gather.11.cloned.1.call-start = ((), (), s32[]{:S(2)}) async-start(), calls=%async_computation.14 | async-start | bytes 1671168 | tf_op jit(solution)/shard_map/all_gather | solution.py:50
  165.8 97.5 %all-gather.13.cloned.1.call-start = ((), (), s32[]{:S(2)}) async-start(), calls=%async_computation.15 | async-start | bytes 1671168 | tf_op jit(solution)/shard_map/all_gather | solution.py:50
  233.3 54.4 %copy-start.1 = (bf16[4,1024,384]{1,2,0:T(8,128)(2,1)S(1)}, bf16[4,1024,384]{1,2,0:T(8,128)(2,1)}, u32[]{:S(2)}) copy-start(bf16[4,1024,384]{1,2,0:T(8,128)(2,1)} %copy.59) | copy-start | bytes 9437188
  233.3 98.4 %all-gather.15.cloned.1.call-start = ((), (), s32[]{:S(2)}) async-start(), calls=%async_computation.16 | async-start | bytes 1671168 | tf_op jit(solution)/shard_map/all_gather | solution.py:50
  301.8 98.3 %all-gather.17.cloned.1.call-start = ((), (), s32[]{:S(2)}) async-start(), calls=%async_computation.17 | async-start | bytes 1671168 | tf_op jit(solution)/shard_map/all_gather | solution.py:50
Sparse Core Ops, SparseCore 0:
  25.8 31.1 all-gather.6
  95.5 29.7 all-gather.8
  165.9 29.7 all-gather.10
  233.4 29.7 all-gather.12
  301.9 29.7 all-gather.14
  370.3 29.7 all-gather.16
where the time goes:
time: 440 us; the launch traced here: 439 us
  waiting for transfers between devices  193 us (44%)
  blocking collectives  124 us (28%)
  matrix products  80.5 us (18%)
  local copies, waits for them, and re-layouts  14.3 us (3%)
  between operations  13.9 us (3%)
  starting transfers between devices  13.2 us (3%)
    all_gather x6, waiting for transfers between devices, apply_reflection(): lax.all_gather(spectrum, 'blk', axis=3, tiled=True)  181 us
    all_to_all x6, blocking collectives, to_spectrum(): lax.all_to_all(spectrum, 'freq', split_axis=2, concat_axis=0, tiled=True)  67.5 us
    dot_general x6, matrix products, apply_reflection(): jnp.einsum('jars,fbjs->fabjr', reflection, lax.all_gather(spectrum, 'blk'...  61.4 us
    all_to_all x4, blocking collectives, to_time(): lax.all_to_all(values, 'freq', split_axis=0, concat_axis=2, tiled=True)  56.1 us
    dot_general x6, matrix products, to_spectrum(): jnp.einsum('kt,ftr->fkr', forward_table, field, preferred_element_type=jn...  15.7 us
    all_to_all x2, starting transfers between devices, to_time(): lax.all_to_all(values, 'freq', split_axis=0, concat_axis=2, tiled=True)  12.8 us
    all_to_all x2, waiting for transfers between devices, to_time(): lax.all_to_all(values, 'freq', split_axis=0, concat_axis=2, tiled=True)  12.6 us
  transfers between devices with their start and end apart: 8, of which 8 were waited for; matrix products, arithmetic and copies ran while one was open for 1% of the time, Pallas kernels for 0%

commit v1 on v0

v1 whole, which is shorter than its diff:
```python
import functools
import math

import jax
import jax.numpy as jnp
import ml_dtypes
import numpy as np
from jax import lax
from jax.experimental import pallas as pl
from jax.experimental.pallas import tpu as pltpu
from jax.sharding import Mesh
from jax.sharding import PartitionSpec as P

ITERS = 3
INNER = 64
OUTER = 80
EDGES = 2 * (OUTER - INNER + 1)
HEAD = 96
TAIL = 80
BF16 = ml_dtypes.bfloat16


def make_tables(count_time, count_freq):
    moments = np.arange(count_time)
    bins = 1 + np.arange(count_freq) * (count_time // (2 * count_freq))
    turns = bins[:, None] * moments[None, :] % count_time
    phase = turns.astype(np.float32) * np.float32(2.0 * math.pi / count_time)
    stacked = np.concatenate([np.cos(phase), -np.sin(phase)], 0).astype(np.float32)
    forward = (stacked * np.float32(count_time ** (-0.5))).astype(BF16)
    inverse = (stacked.T * np.float32(math.sqrt(2.0 / count_freq))).astype(BF16)
    return forward.astype(np.float64), inverse.astype(np.float64)


def spread(matrix, count):
    return np.kron(matrix, np.eye(count)).astype(BF16)


def make_constants(count_time, count_freq, groups, focal_local, sub):
    forward, inverse = make_tables(count_time, count_freq)
    local_freq = count_freq // groups
    order = np.array(
        [c * count_freq + g * local_freq + j for g in range(groups) for j in range(local_freq) for c in range(2)]
    )
    forward, inverse = forward[order], inverse[:, order]
    inside = np.array(list(range(INNER)) + list(range(count_time - INNER + 1, count_time)))
    edge = np.array(list(range(INNER, OUTER + 1)) + [count_time - s for s in range(INNER, OUTER + 1)])
    core = forward[:, inside] @ inverse[inside]
    high = core.astype(BF16).astype(np.float64)
    low = core - high
    per = 2 * local_freq
    to_edge = spread(inverse[edge], sub)
    mix, back = [], []
    for g in range(groups):
        rows = slice(g * per, (g + 1) * per)
        mix.append(np.concatenate([spread(high[rows], sub), spread(low[rows], sub)], 0))
        back.append(spread(forward[rows][:, edge], sub))
    first = np.einsum("kt,fg->kfgt", forward, np.eye(focal_local)).reshape(
        2 * count_freq * focal_local, focal_local * count_time
    )
    window_rows = np.array(list(range(HEAD)) + list(range(count_time - TAIL, count_time)))
    last = np.einsum("tk,fg->ftkg", inverse[window_rows], np.eye(focal_local)).reshape(
        focal_local * (HEAD + TAIL), 2 * count_freq * focal_local
    )
    return to_edge, np.stack(mix), np.stack(back), first.astype(BF16), last.astype(BF16)


def product_kernel(orient, copies, core_ref, r_ref, own_ref, other_ref, out_ref, acc_ref):
    step = pl.program_id(0)
    local_freq, _, rows, _ = r_ref.shape
    wide = own_ref.shape[1] // local_freq

    @pl.when(step == 0)
    def _():
        acc_ref[...] = jnp.zeros_like(acc_ref)

    first = core_ref[0] == 0
    own, other = own_ref[0], other_ref[0]
    x = jnp.concatenate([jnp.where(first, own, other), jnp.where(first, other, own)], axis=1)
    for j in range(local_freq):
        matrix = r_ref[j].reshape(2 * rows, r_ref.shape[3])
        acc_ref[j] += lax.dot_general(
            x[j * wide : (j + 1) * wide],
            matrix,
            (((1,), (1,)), ((), ())),
            preferred_element_type=jnp.float32,
        )

    @pl.when(step == pl.num_programs(0) - 1)
    def _():
        half = wide // 2
        for j in range(local_freq):
            real = acc_ref[j, :half, :rows] - orient * acc_ref[j, half:, rows:]
            imag = acc_ref[j, half:, :rows] + orient * acc_ref[j, :half, rows:]
            both = jnp.concatenate([real, imag], 0).astype(jnp.bfloat16)
            for d in range(copies):
                out_ref[d, j * wide : (j + 1) * wide] = both


def product(reflection, own, other, core, orient, copies):
    local_freq, _, rows, order = reflection.shape
    blocks, wide, _ = own.shape
    return pl.pallas_call(
        functools.partial(product_kernel, orient, copies),
        out_shape=jax.ShapeDtypeStruct((copies, wide, rows), jnp.bfloat16),
        grid_spec=pltpu.PrefetchScalarGridSpec(
            num_scalar_prefetch=1,
            grid=(blocks,),
            in_specs=[
                pl.BlockSpec((local_freq, 2, rows, order // blocks), lambda k, c: (0, 0, 0, k)),
                pl.BlockSpec((1, wide, rows), lambda k, c: (k, 0, 0)),
                pl.BlockSpec((1, wide, rows), lambda k, c: (k, 0, 0)),
            ],
            out_specs=pl.BlockSpec((copies, wide, rows), lambda k, c: (0, 0, 0)),
            scratch_shapes=[pltpu.VMEM((local_freq, wide // local_freq, 2 * rows), jnp.float32)],
        ),
        compiler_params=pltpu.CompilerParams(
            dimension_semantics=("arbitrary",), vmem_limit_bytes=24 << 20
        ),
        cost_estimate=pl.CostEstimate(
            flops=4 * reflection.size * wide // local_freq,
            bytes_accessed=2 * reflection.size,
            transcendentals=0,
        ),
    )(core, reflection, own, other)


def mixing_kernel(subtract, copies, v_ref, edge_ref, mix_ref, back_ref, onset_ref, start_ref, out_ref):
    total, focal, rows = v_ref.shape
    per = start_ref.shape[0]
    sub = edge_ref.shape[1] // total
    wide = per * sub
    for g in range(focal // sub):
        part = slice(g * sub, (g + 1) * sub)
        v = v_ref[:, part, :].reshape(total * sub, rows)
        at_edge = jnp.dot(edge_ref[...], v, preferred_element_type=jnp.float32)
        at_edge = at_edge.reshape(EDGES, sub, rows)
        number = lax.broadcasted_iota(jnp.int32, (EDGES, sub, rows), 0)
        time = INNER + jnp.where(number < EDGES // 2, number, number - EDGES // 2)
        kept = jnp.where(time < onset_ref[part, :][None], at_edge, 0.0).astype(jnp.bfloat16)
        both = jnp.dot(mix_ref[...], v, preferred_element_type=jnp.float32)
        result = both[:wide] + both[wide:]
        result += jnp.dot(
            back_ref[...], kept.reshape(EDGES * sub, rows), preferred_element_type=jnp.float32
        )
        result = result.reshape(per, sub, rows)
        if subtract:
            result = start_ref[:, part, :].astype(jnp.float32) - result
        result = result.astype(jnp.bfloat16)
        for d in range(copies):
            out_ref[d, :, part, :] = result


def mixing(values, tables, onset, start, subtract, copies):
    per, focal, rows = start.shape
    return pl.pallas_call(
        functools.partial(mixing_kernel, subtract, copies),
        out_shape=jax.ShapeDtypeStruct((copies, per, focal, rows), jnp.bfloat16),
        compiler_params=pltpu.CompilerParams(vmem_limit_bytes=24 << 20),
    )(values.reshape(-1, focal, rows), *tables, onset, start)


def shards(reflection, direct_focus, onset):
    groups = lax.axis_size("freq")
    pairs = lax.axis_size("pair")
    local_freq = reflection.shape[0]
    per = 2 * local_freq
    focal_local, count_time, rows = direct_focus.shape
    focal = focal_local * groups
    sub = 16
    to_edge, mix, back, first, last = make_constants(
        count_time, local_freq * groups, groups, focal_local, sub
    )
    here = lax.axis_index("freq")
    tables = (
        jnp.asarray(to_edge),
        lax.dynamic_index_in_dim(jnp.asarray(mix), here, 0, keepdims=False),
        lax.dynamic_index_in_dim(jnp.asarray(back), here, 0, keepdims=False),
    )
    core = lax.axis_index("core").astype(jnp.int32).reshape(1)

    def over(axis, value):
        return lax.all_to_all(value, axis, split_axis=0, concat_axis=0, tiled=True)

    def swap(value):
        return lax.ppermute(value, "core", [(0, 1), (1, 0)])

    def apply_reflection(spread_spectrum, orient, copies):
        own = over("pair", spread_spectrum)
        return product(reflection, own, swap(own), core, orient, copies)

    spectrum = jnp.dot(
        jnp.asarray(first),
        direct_focus.reshape(focal_local * count_time, rows),
        preferred_element_type=jnp.float32,
    ).astype(jnp.bfloat16)
    spectrum = spectrum.reshape(groups, per, focal_local, rows)
    levels = jnp.broadcast_to(
        onset.astype(jnp.bfloat16)[None, None], (groups, 1, focal_local, rows)
    )
    sent = jnp.concatenate([spectrum, levels], 1).reshape(groups, (per + 1) * focal_local, rows)
    got = over("freq", sent).reshape(groups, per + 1, focal_local, rows)
    got = jnp.swapaxes(got, 0, 1).reshape(per + 1, focal, rows)
    start, all_onset = got[:per], got[per].astype(jnp.int32)

    moving = jnp.broadcast_to(start.reshape(1, per * focal, rows), (pairs, per * focal, rows))
    for repeat in range(ITERS):
        values = apply_reflection(moving, 1.0, groups)
        values = over("freq", values)
        moving = mixing(values, tables, all_onset, start, False, pairs)
        moving = moving.reshape(pairs, per * focal, rows)
        if repeat < ITERS - 1:
            values = apply_reflection(moving, -1.0, groups)
            values = over("freq", values)
            moving = mixing(values, tables, all_onset, start, True, pairs)
            moving = moving.reshape(pairs, per * focal, rows)
    values = apply_reflection(moving, -1.0, 1)
    values = values.reshape(per, groups, focal_local, rows)
    values = jnp.swapaxes(values, 0, 1).reshape(groups, per * focal_local, rows)
    values = over("freq", values).reshape(groups * per * focal_local, rows)
    change = jnp.dot(jnp.asarray(last), values, preferred_element_type=jnp.float32)
    change = change.reshape(focal_local, HEAD + TAIL, rows)
    number = jnp.arange(HEAD + TAIL)
    distance = jnp.where(number < HEAD, number, HEAD + TAIL - number)
    change = jnp.where(distance[None, :, None] < onset[:, None, :], change, 0.0)

    def finish(part, piece):
        return (part.astype(jnp.float32) - piece).astype(jnp.bfloat16)

    return jnp.concatenate(
        [
            finish(direct_focus[:, :HEAD], change[:, :HEAD]),
            direct_focus[:, HEAD : count_time - TAIL],
            finish(direct_focus[:, count_time - TAIL :], change[:, HEAD:]),
        ],
        1,
    )


def solution(mesh):
    groups, blocks = mesh.devices.shape
    split = Mesh(mesh.devices.reshape(groups, blocks // 2, 2), ("freq", "pair", "core"))
    rows = ("pair", "core")
    return jax.shard_map(
        shards,
        mesh=split,
        in_specs=(P("freq", None, rows, None), P("freq", None, rows), P("freq", rows)),
        out_specs=P("freq", None, rows),
        check_vma=False,
    )
```

time: 440 us -> 296 us (0.67)
  waiting for transfers between devices: 193 us -> 31.2 us
  matrix products: 80.5 us -> 3.2 us
  Pallas kernels: 0 us -> 54.9 us
  blocking collectives: 124 us -> 176 us
  between operations: 13.9 us -> 0.26 us
  starting transfers between devices: 13.2 us -> 8.33 us
    all_gather x6 -> x0, waiting for transfers between devices: 181 us -> none  [apply_reflection(): lax.all_gather(spectrum, 'blk', axis=3, tiled=True)]
    dot_general x13 -> x2, matrix products: 80.5 us -> 3.2 us  [the longest x1 2.92 us: shards(): jnp.dot(jnp.asarray(first), direct_focus.reshape(focal_local * count_time...]
    pallas_call x0 -> x11, Pallas kernels: none -> 54.9 us  [the longest x6 49.2 us: product(): pl.pallas_call(functools.partial(product_kernel, orient, copies), out_sha...]
    all_to_all x10 -> x11, blocking collectives: 124 us -> 176 us  [over(): return lax.all_to_all(value, axis, split_axis=0, concat_axis=0, tiled=True)]
    ppermute x0 -> x6, waiting for transfers between devices: none -> 11.9 us  [swap(): return lax.ppermute(value, 'core', [(0, 1), (1, 0)])]
    unnamed x15 -> x16, local copies, waits for them, and re-layouts: 2.89 us -> 12.8 us
    all_to_all x2, waiting for transfers between devices: 12.6 us -> 19.3 us  [over(): return lax.all_to_all(value, axis, split_axis=0, concat_axis=0, tiled=True)]
    convert_element_type x7 -> x2, local copies, waits for them, and re-layouts: 5.14 us -> 0.03 us  [shards(): start, all_onset = (got[:per], got[per].astype(jnp.int32))]
where the time goes in v1:
time: 296 us
  blocking collectives  176 us (59%)
  Pallas kernels  54.9 us (19%)
  waiting for transfers between devices  31.2 us (11%)
  local copies, waits for them, and re-layouts  17.3 us (6%)
  starting transfers between devices  8.33 us (3%)
  other arithmetic  4.74 us (2%)
  matrix products  3.2 us (1%)
    all_to_all x11, blocking collectives, over(): return lax.all_to_all(value, axis, split_axis=0, concat_axis=0, tiled=True)  176 us
    pallas_call x6, Pallas kernels, product(): pl.pallas_call(functools.partial(product_kernel, orient, copies), out_sha...  49.2 us
    all_to_all x2, waiting for transfers between devices, over(): return lax.all_to_all(value, axis, split_axis=0, concat_axis=0, tiled=True)  19.3 us
    unnamed x16, local copies, waits for them, and re-layouts  12.8 us
    ppermute x6, waiting for transfers between devices, swap(): return lax.ppermute(value, 'core', [(0, 1), (1, 0)])  11.9 us
    all_to_all x2, starting transfers between devices, over(): return lax.all_to_all(value, axis, split_axis=0, concat_axis=0, tiled=True)  8.31 us
  transfers between devices with their start and end apart: 8, of which 8 were waited for; matrix products, arithmetic and copies ran while one was open for 1% of the time, Pallas kernels for 0%

profile of v1, /device:TPU:0, one launch (start us, length us, event | category | flops | bytes accessed | tf_op | source)
XLA Modules:
  0.0 295.5 jit_solution(10629671644779865650)
XLA Ops:
  0.7 2.9 convolution_convert_fusion
  3.8 15.5 %all_to_all.65 = bf16[8,20,384]{2,1,0:T(8,128)(2,1)S(1)} all-to-all(bf16[8,20,384]{2,1,0:T(8,128)(2,1)S(1)} %copy.20), channel_id=1, replica_groups=mesh['freq'=8,'pair'=8,'core'=2] {'freq'}, dimensions={0} | all-to-all | bytes 245760 | tf_op jit(solution)/shard_map/all_to_all | solution.py:182
  19.4 15.8 %all_to_all.66.own_ref = bf16[8,128,384]{2,1,0:T(8,128)(2,1)S(1)} all-to-all(bf16[8,128,384]{2,1,0:T(8,128)(2,1)S(1)} %broadcast_in_dim.21), channel_id=1, replica_groups=mesh['freq'=8,'pair'=8,'core'=2] {'pair'}, dimensions={0} | all-to-all | bytes 1572864 | tf_op jit(solution)/shard_map/all_to_all | solution.py:182
  35.3 2.3 collective-permute-done.other_ref
  37.5 6.4 %copy-done = bf16[2,2,384,6144]{3,2,1,0:T(8,128)(2,1)S(1)} copy-done((bf16[2,2,384,6144]{3,2,1,0:T(8,128)(2,1)S(1)}, bf16[2,2,384,6144]{3,2,1,0:T(8,128)(2,1)}, u32[]{:S(2)}) %copy-start) | copy-done | bytes 18874392
  43.9 8.9 %shard_map.82 = bf16[8,128,384]{2,1,0:T(8,128)(2,1)} custom-call(s32[1]{0:T(128)} %bitcast.core_ref, bf16[2,2,384,6144]{3,2,1,0:T(8,128)(2,1)S(1)} %copy-done, bf16[8,128,384]{2,1,0:T(8,128)(2,1)S(1)} %all_to_all.66.own_ref, bf16[8,128,384]{2,1,0:T(8,128)(2,1)S(1)} %collective-permute-done.other_ref), custom_call_target="tpu_custom_call" | custom-call | flops 2415919104 | bytes 18874368 | tf_op jit(solution)/shard_map/pallas_call | solution.py:102
  52.8 3.8 %all-to-all-start.2 = ((bf16[8,128,384]{2,1,0:T(8,128)(2,1)}), bf16[8,128,384]{2,1,0:T(8,128)(2,1)S(1)}, u32[]{:S(2)}, u32[]{:S(2)}) async-start(bf16[8,128,384]{2,1,0:T(8,128)(2,1)} %shard_map.82), calls=%async_computation.2 | async-start | bytes 1572864 | tf_op jit(solution)/shard_map/all_to_all | solution.py:182
  58.6 11.5 %all-to-all-done.2 = bf16[8,128,384]{2,1,0:T(8,128)(2,1)S(1)} async-done(((bf16[8,128,384]{2,1,0:T(8,128)(2,1)}), bf16[8,128,384]{2,1,0:T(8,128)(2,1)S(1)}, u32[]{:S(2)}, u32[]{:S(2)}) %all-to-all-start.2) | async-done | bytes 786464 | tf_op jit(solution)/shard_map/all_to_all | solution.py:182
  71.2 15.1 %all_to_all.67.own_ref = bf16[8,128,384]{2,1,0:T(8,128)(2,1)S(1)} all-to-all(bf16[8,128,384]{2,1,0:T(8,128)(2,1)S(1)} %bitcast.32), channel_id=1, replica_groups=mesh['freq'=8,'pair'=8,'core'=2] {'pair'}, dimensions={0} | all-to-all | bytes 1572864 | tf_op jit(solution)/shard_map/all_to_all | solution.py:182
  86.3 2.3 collective-permute-done.1.other_ref
  88.6 6.4 %copy-done.1 = bf16[2,2,384,6144]{3,2,1,0:T(8,128)(2,1)S(1)} copy-done((bf16[2,2,384,6144]{3,2,1,0:T(8,128)(2,1)S(1)}, bf16[2,2,384,6144]{3,2,1,0:T(8,128)(2,1)}, u32[]{:S(2)}) %copy-start.1) | copy-done | bytes 18874392
  95.0 8.1 %shard_map.84 = bf16[8,128,384]{2,1,0:T(8,128)(2,1)S(1)} custom-call(s32[1]{0:T(128)} %bitcast.core_ref, bf16[2,2,384,6144]{3,2,1,0:T(8,128)(2,1)S(1)} %copy-done.1, bf16[8,128,384]{2,1,0:T(8,128)(2,1)S(1)} %all_to_all.67.own_ref, bf16[8,128,384]{2,1,0:T(8,128)(2,1)S(1)} %collective-permute-done.1.other_ref), custom_call_target="tpu_custom_call" | custom-call | flops 2415919104 | bytes 18874368 | tf_op jit(solution)/shard_map/pallas_call | solution.py:102
  103.0 18.6 %all_to_all.68 = bf16[8,128,384]{2,1,0:T(8,128)(2,1)S(1)} all-to-all(bf16[8,128,384]{2,1,0:T(8,128)(2,1)S(1)} %shard_map.84), channel_id=1, replica_groups=mesh['freq'=8,'pair'=8,'core'=2] {'freq'}, dimensions={0} | all-to-all | bytes 1572864 | tf_op jit(solution)/shard_map/all_to_all | solution.py:182
  121.7 1.1 shard_map.85
  122.8 13.7 %all_to_all.69.own_ref = bf16[8,128,384]{2,1,0:T(8,128)(2,1)S(1)} all-to-all(bf16[8,128,384]{2,1,0:T(8,128)(2,1)S(1)} %bitcast.34), channel_id=1, replica_groups=mesh['freq'=8,'pair'=8,'core'=2] {'pair'}, dimensions={0} | all-to-all | bytes 1572864 | tf_op jit(solution)/shard_map/all_to_all | solution.py:182
  136.5 2.3 collective-permute-done.2.other_ref
  138.8 8.1 %shard_map.86 = bf16[8,128,384]{2,1,0:T(8,128)(2,1)S(1)} custom-call(s32[1]{0:T(128)} %bitcast.core_ref, bf16[2,2,384,6144]{3,2,1,0:T(8,128)(2,1)S(1)} %copy-done.2, bf16[8,128,384]{2,1,0:T(8,128)(2,1)S(1)} %all_to_all.69.own_ref, bf16[8,128,384]{2,1,0:T(8,128)(2,1)S(1)} %collective-permute-done.2.other_ref), custom_call_target="tpu_custom_call" | custom-call | flops 2415919104 | bytes 18874368 | tf_op jit(solution)/shard_map/pallas_call | solution.py:102
  146.8 18.5 %all_to_all.70 = bf16[8,128,384]{2,1,0:T(8,128)(2,1)S(1)} all-to-all(bf16[8,128,384]{2,1,0:T(8,128)(2,1)S(1)} %shard_map.86), channel_id=1, replica_groups=mesh['freq'=8,'pair'=8,'core'=2] {'freq'}, dimensions={0} | all-to-all | bytes 1572864 | tf_op jit(solution)/shard_map/all_to_all | solution.py:182
  166.5 13.7 %all_to_all.71.own_ref = bf16[8,128,384]{2,1,0:T(8,128)(2,1)S(1)} all-to-all(bf16[8,128,384]{2,1,0:T(8,128)(2,1)S(1)} %bitcast.36), channel_id=1, replica_groups=mesh['freq'=8,'pair'=8,'core'=2] {'pair'}, dimensions={0} | all-to-all | bytes 1572864 | tf_op jit(solution)/shard_map/all_to_all | solution.py:182
  180.2 2.3 collective-permute-done.3.other_ref
  182.5 8.1 %shard_map.88 = bf16[8,128,384]{2,1,0:T(8,128)(2,1)S(1)} custom-call(s32[1]{0:T(128)} %bitcast.core_ref, bf16[2,2,384,6144]{3,2,1,0:T(8,128)(2,1)S(1)} %copy-done.2, bf16[8,128,384]{2,1,0:T(8,128)(2,1)S(1)} %all_to_all.71.own_ref, bf16[8,128,384]{2,1,0:T(8,128)(2,1)S(1)} %collective-permute-done.3.other_ref), custom_call_target="tpu_custom_call" | custom-call | flops 2415919104 | bytes 18874368 | tf_op jit(solution)/shard_map/pallas_call | solution.py:102
  190.5 18.5 %all_to_all.72 = bf16[8,128,384]{2,1,0:T(8,128)(2,1)S(1)} all-to-all(bf16[8,128,384]{2,1,0:T(8,128)(2,1)S(1)} %shard_map.88), channel_id=1, replica_groups=mesh['freq'=8,'pair'=8,'core'=2] {'freq'}, dimensions={0} | all-to-all | bytes 1572864 | tf_op jit(solution)/shard_map/all_to_all | solution.py:182
  210.2 13.7 %all_to_all.73.own_ref = bf16[8,128,384]{2,1,0:T(8,128)(2,1)S(1)} all-to-all(bf16[8,128,384]{2,1,0:T(8,128)(2,1)S(1)} %bitcast.38), channel_id=1, replica_groups=mesh['freq'=8,'pair'=8,'core'=2] {'pair'}, dimensions={0} | all-to-all | bytes 1572864 | tf_op jit(solution)/shard_map/all_to_all | solution.py:182
  223.9 2.3 collective-permute-done.4.other_ref
  226.2 8.1 %shard_map.90 = bf16[8,128,384]{2,1,0:T(8,128)(2,1)S(1)} custom-call(s32[1]{0:T(128)} %bitcast.core_ref, bf16[2,2,384,6144]{3,2,1,0:T(8,128)(2,1)S(1)} %copy-done.2, bf16[8,128,384]{2,1,0:T(8,128)(2,1)S(1)} %all_to_all.73.own_ref, bf16[8,128,384]{2,1,0:T(8,128)(2,1)S(1)} %collective-permute-done.4.other_ref), custom_call_target="tpu_custom_call" | custom-call | flops 2415919104 | bytes 18874368 | tf_op jit(solution)/shard_map/pallas_call | solution.py:102
  234.2 18.8 %all_to_all.74 = bf16[8,128,384]{2,1,0:T(8,128)(2,1)S(1)} all-to-all(bf16[8,128,384]{2,1,0:T(8,128)(2,1)S(1)} %shard_map.90), channel_id=1, replica_groups=mesh['freq'=8,'pair'=8,'core'=2] {'freq'}, dimensions={0} | all-to-all | bytes 1572864 | tf_op jit(solution)/shard_map/all_to_all | solution.py:182
  254.2 13.7 %all_to_all.75.own_ref = bf16[8,128,384]{2,1,0:T(8,128)(2,1)S(1)} all-to-all(bf16[8,128,384]{2,1,0:T(8,128)(2,1)S(1)} %bitcast.31), channel_id=1, replica_groups=mesh['freq'=8,'pair'=8,'core'=2] {'pair'}, dimensions={0} | all-to-all | bytes 1572864 | tf_op jit(solution)/shard_map/all_to_all | solution.py:182
  267.9 1.7 slice.30
  270.1 8.0 %shard_map.92 = bf16[1,128,384]{2,1,0:T(8,128)(2,1)S(1)} custom-call(s32[1]{0:T(128)} %bitcast.core_ref, bf16[2,2,384,6144]{3,2,1,0:T(8,128)(2,1)S(1)} %copy-done.2, bf16[8,128,384]{2,1,0:T(8,128)(2,1)S(1)} %all_to_all.75.own_ref, bf16[8,128,384]{2,1,0:T(8,128)(2,1)S(1)} %collective-permute-done.5.other_ref), custom_call_target="tpu_custom_call" | custom-call | flops 2415919104 | bytes 18874368 | tf_op jit(solution)/shard_map/pallas_call | solution.py:102
  278.9 4.5 %all-to-all-start.12 = ((bf16[8,16,384]{2,1,0:T(8,128)(2,1)}), bf16[8,16,384]{2,1,0:T(8,128)(2,1)S(1)}, u32[]{:S(2)}, u32[]{:S(2)}) async-start(bf16[8,16,384]{2,1,0:T(8,128)(2,1)} %copy.26), calls=%async_computation.12 | async-start | bytes 196608 | tf_op jit(solution)/shard_map/all_to_all | solution.py:182
  283.4 7.8 %all-to-all-done.12 = bf16[8,16,384]{2,1,0:T(8,128)(2,1)S(1)} async-done(((bf16[8,16,384]{2,1,0:T(8,128)(2,1)}), bf16[8,16,384]{2,1,0:T(8,128)(2,1)S(1)}, u32[]{:S(2)}, u32[]{:S(2)}) %all-to-all-start.12) | async-done | bytes 98336 | tf_op jit(solution)/shard_map/all_to_all | solution.py:182
  293.7 1.8 pad_maximum_fusion
  (50 shorter events, 11.1 us)
Async XLA Ops:
  35.3 2.3 collective-permute-start
  37.5 6.4 %copy-start = (bf16[2,2,384,6144]{3,2,1,0:T(8,128)(2,1)S(1)}, bf16[2,2,384,6144]{3,2,1,0:T(8,128)(2,1)}, u32[]{:S(2)}) copy-start(bf16[2,2,384,6144]{3,2,1,0:T(8,128)(2,1)} %r_ref.11) | copy-start | bytes 56623108
  43.9 26.2 %copy-start.3 = (bf16[544,512]{1,0:T(8,128)(2,1)S(1)}, bf16[544,512]{1,0:T(8,128)(2,1)}, u32[]{:S(2)}) copy-start(bf16[544,512]{1,0:T(8,128)(2,1)} %constant.36.clone.edge_ref) | copy-start | bytes 1671172
  52.8 17.2 %all-to-all-start.2 = ((bf16[8,128,384]{2,1,0:T(8,128)(2,1)}), bf16[8,128,384]{2,1,0:T(8,128)(2,1)S(1)}, u32[]{:S(2)}, u32[]{:S(2)}) async-start(bf16[8,128,384]{2,1,0:T(8,128)(2,1)} %shard_map.82), calls=%async_computation.2 | async-start | bytes 1572864 | tf_op jit(solution)/shard_map/all_to_all | solution.py:182
  86.3 2.3 collective-permute-start.1
  88.6 6.4 %copy-start.1 = (bf16[2,2,384,6144]{3,2,1,0:T(8,128)(2,1)S(1)}, bf16[2,2,384,6144]{3,2,1,0:T(8,128)(2,1)}, u32[]{:S(2)}) copy-start(bf16[2,2,384,6144]{3,2,1,0:T(8,128)(2,1)} %r_ref.11) | copy-start | bytes 56623108
  95.0 43.8 %copy-start.2 = (bf16[2,2,384,6144]{3,2,1,0:T(8,128)(2,1)S(1)}, bf16[2,2,384,6144]{3,2,1,0:T(8,128)(2,1)}, u32[]{:S(2)}) copy-start(bf16[2,2,384,6144]{3,2,1,0:T(8,128)(2,1)} %r_ref.11) | copy-start | bytes 56623108
  136.5 2.3 collective-permute-start.2
  180.2 2.3 collective-permute-start.3
  223.9 2.3 collective-permute-start.4
  234.2 33.6 %copy-start.4 = (bf16[4,1024,384]{2,1,0:T(8,128)(2,1)S(1)}, bf16[4,1024,384]{2,1,0:T(8,128)(2,1)}, u32[]{:S(2)}) copy-start(bf16[4,1024,384]{2,1,0:T(8,128)(2,1)} %param.9) | copy-start | bytes 9437188
  267.8 2.3 collective-permute-start.5
  269.6 21.6 %copy-start.6 = (bf16[704,128]{1,0:T(8,128)(2,1)S(1)}, bf16[704,128]{1,0:T(8,128)(2,1)}, u32[]{:S(2)}) copy-start(bf16[704,128]{1,0:T(8,128)(2,1)} %constant.40.clone) | copy-start | bytes 540676
  269.6 21.9 %copy-start.7 = (s32[4,384]{1,0:T(4,128)S(1)}, s32[4,384]{1,0:T(4,128)}, u32[]{:S(2)}) copy-start(s32[4,384]{1,0:T(4,128)} %param.10) | copy-start | bytes 18436
  278.2 15.5 %copy-start.5 = (bf16[4,848,384]{2,1,0:T(8,128)(2,1)S(1)}, bf16[4,848,384]{2,1,0:T(8,128)(2,1)}, u32[]{:S(2)}) copy-start(bf16[4,848,384]{2,1,0:T(8,128)(2,1)} %slice.30) | copy-start | bytes 7815172
  278.9 12.3 %all-to-all-start.12 = ((bf16[8,16,384]{2,1,0:T(8,128)(2,1)}), bf16[8,16,384]{2,1,0:T(8,128)(2,1)S(1)}, u32[]{:S(2)}, u32[]{:S(2)}) async-start(bf16[8,16,384]{2,1,0:T(8,128)(2,1)} %copy.26), calls=%async_computation.12 | async-start | bytes 196608 | tf_op jit(solution)/shard_map/all_to_all | solution.py:182

commit v2 on v0

v2 whole, which is shorter than its diff:
```python
import functools
import math

import jax
import jax.numpy as jnp
import ml_dtypes
import numpy as np
from jax import lax
from jax.experimental import pallas as pl
from jax.experimental.pallas import tpu as pltpu
from jax.sharding import Mesh
from jax.sharding import PartitionSpec as P

ITERS = 3
INNER = 64
OUTER = 80
EDGES = 2 * (OUTER - INNER + 1)
HEAD = 96
TAIL = 80
BF16 = ml_dtypes.bfloat16


def make_tables(count_time, count_freq):
    moments = np.arange(count_time)
    bins = 1 + np.arange(count_freq) * (count_time // (2 * count_freq))
    turns = bins[:, None] * moments[None, :] % count_time
    phase = turns.astype(np.float32) * np.float32(2.0 * math.pi / count_time)
    stacked = np.concatenate([np.cos(phase), -np.sin(phase)], 0).astype(np.float32)
    forward = (stacked * np.float32(count_time ** (-0.5))).astype(BF16)
    inverse = (stacked.T * np.float32(math.sqrt(2.0 / count_freq))).astype(BF16)
    return forward.astype(np.float64), inverse.astype(np.float64)


def spread(matrix, count):
    return np.kron(matrix, np.eye(count)).astype(BF16)


def make_constants(count_time, count_freq, groups, sets, focal_local, sub):
    forward, inverse = make_tables(count_time, count_freq)
    local_freq = count_freq // groups
    order = np.array(
        [c * count_freq + g * local_freq + j for g in range(groups) for j in range(local_freq) for c in range(2)]
    )
    forward, inverse = forward[order], inverse[:, order]
    inside = np.array(list(range(INNER)) + list(range(count_time - INNER + 1, count_time)))
    edge = np.array(list(range(INNER, OUTER + 1)) + [count_time - s for s in range(INNER, OUTER + 1)])
    core = forward[:, inside] @ inverse[inside]
    high = core.astype(BF16).astype(np.float64)
    low = core - high
    per = 2 * count_freq // sets
    to_edge = spread(inverse[edge], sub)
    mix, back = [], []
    for g in range(sets):
        rows = slice(g * per, (g + 1) * per)
        mix.append(np.concatenate([spread(high[rows], sub), spread(low[rows], sub)], 0))
        back.append(spread(forward[rows][:, edge], sub))
    first = np.einsum("kt,fg->kfgt", forward, np.eye(focal_local)).reshape(
        2 * count_freq * focal_local, focal_local * count_time
    )
    window_rows = np.array(list(range(HEAD)) + list(range(count_time - TAIL, count_time)))
    last = np.einsum("tk,fg->ftkg", inverse[window_rows], np.eye(focal_local)).reshape(
        focal_local * (HEAD + TAIL), 2 * count_freq * focal_local
    )
    return to_edge, np.stack(mix), np.stack(back), first.astype(BF16), last.astype(BF16)


def opening_kernel(set_ref, first_ref, direct_ref, mix_ref, back_ref, out_ref, mix_out, back_out, first_in, direct_in, sems):
    focal_local, count_time, _ = direct_ref.shape
    here = set_ref[0]
    tables = [
        pltpu.make_async_copy(mix_ref.at[here], mix_out, sems.at[0]),
        pltpu.make_async_copy(back_ref.at[here], back_out, sems.at[1]),
    ]
    fetch = [pltpu.make_async_copy(first_ref, first_in, sems.at[2])]
    fetch += [
        pltpu.make_async_copy(direct_ref.at[f], direct_in.at[f], sems.at[3 + f])
        for f in range(focal_local)
    ]
    for copy in fetch + tables:
        copy.start()
    fetch[0].wait()
    total = jnp.zeros((first_in.shape[0], direct_in.shape[2]), jnp.float32)
    for f in range(focal_local):
        fetch[1 + f].wait()
        total += jnp.dot(
            first_in[:, f * count_time : (f + 1) * count_time],
            direct_in[f],
            preferred_element_type=jnp.float32,
        )
    groups, copies, chunk, _ = out_ref.shape
    for g in range(groups):
        piece = total[g * chunk : (g + 1) * chunk].astype(jnp.bfloat16)
        for d in range(copies):
            out_ref[g, d] = piece
    for copy in tables:
        copy.wait()


def opening(first, direct_focus, mix, back, here, groups, copies):
    focal_local, count_time, rows = direct_focus.shape
    shape = (groups, copies, first.shape[0] // groups, rows)
    whole = pl.BlockSpec(memory_space=pltpu.HBM)
    local = pl.BlockSpec(memory_space=pltpu.VMEM)
    return pl.pallas_call(
        opening_kernel,
        out_shape=[
            jax.ShapeDtypeStruct(shape, jnp.bfloat16),
            jax.ShapeDtypeStruct(mix.shape[1:], jnp.bfloat16),
            jax.ShapeDtypeStruct(back.shape[1:], jnp.bfloat16),
        ],
        in_specs=[pl.BlockSpec(memory_space=pltpu.SMEM)] + [whole] * 4,
        out_specs=[local] * 3,
        scratch_shapes=[
            pltpu.VMEM(first.shape, jnp.bfloat16),
            pltpu.VMEM(direct_focus.shape, jnp.bfloat16),
            pltpu.SemaphoreType.DMA((3 + focal_local,)),
        ],
        compiler_params=pltpu.CompilerParams(vmem_limit_bytes=60 << 20),
        cost_estimate=pl.CostEstimate(
            flops=2 * first.size * rows,
            bytes_accessed=2 * (direct_focus.size + first.size),
            transcendentals=0,
        ),
    )(here, first, direct_focus, mix, back)


def part_of(ref, pairs, halves, first, j, p):
    count, wide, _ = ref.shape
    outer = count // pairs
    size = wide // 2
    pieces = [ref[o * pairs + p, j * size : (j + 1) * size] for o in range(outer)]
    return jnp.concatenate(pieces, 0)


def partial_product(r_ref, x_ref, core, steps, pairs, halves, first, j, total):
    rows = x_ref.shape[2]
    for p in steps:
        matrix, x = [], []
        for q in (p, p + 1):
            column = pl.multiple_of((2 * q + core) * rows, 128)
            matrix.append(r_ref[j, :, :, pl.ds(column, rows)].reshape(2 * rows, rows))
            x.append(part_of(x_ref, pairs, halves, first, j, q))
        total += lax.dot_general(
            jnp.concatenate(matrix, 1),
            jnp.concatenate(x, 1),
            (((1,), (1,)), ((), ())),
            preferred_element_type=jnp.float32,
        )
    return total


def own_kernel(pairs, halves, first, core_ref, r_ref, x_ref, sum_ref):
    for j in range(sum_ref.shape[0]):
        zero = jnp.zeros(sum_ref.shape[1:], jnp.float32)
        sum_ref[j] = partial_product(
            r_ref, x_ref, core_ref[0], range(0, pairs, 2), pairs, halves, first, j, zero
        )


def fetch_kernel(pairs, halves, core_ref, r_ref, x_ref, sum_ref, out_ref, sems):
    count = sems.shape[0]
    wide = r_ref.shape[3] // count
    copies = [
        pltpu.make_async_copy(
            r_ref.at[:, :, :, n * wide : (n + 1) * wide],
            out_ref.at[:, :, :, n * wide : (n + 1) * wide],
            sems.at[n],
        )
        for n in range(count)
    ]
    for copy in copies:
        copy.start()
    sum_ref[...] = jnp.zeros_like(sum_ref)
    step = pairs // count
    for n in range(count):
        copies[n].wait()
        for j in range(sum_ref.shape[0]):
            sum_ref[j] = partial_product(
                out_ref, x_ref, core_ref[0], range(n * step, (n + 1) * step, 2), pairs, halves, True, j, sum_ref[j]
            )


def other_kernel(pairs, halves, sets, orient, kind, *refs):
    core_ref, r_ref, x_ref, sum_ref, extra_ref, out_ref = refs[:6]
    first = kind == "first"
    rows = x_ref.shape[2]
    local_freq, _, columns = sum_ref.shape
    part = columns // halves
    sub = part // 2
    few = sub // sets
    for j in range(local_freq):
        total = partial_product(
            r_ref, x_ref, 1 - core_ref[0], range(0, pairs, 2), pairs, halves, first, j, sum_ref[j]
        )
        turned = total.T
        if first:
            turned = jnp.concatenate(
                [
                    turned[((x * halves + h) * 2 + c) * few : ((x * halves + h) * 2 + c + 1) * few]
                    for h in range(halves)
                    for c in range(2)
                    for x in range(sets)
                ],
                0,
            )
        for h in range(halves):
            real_in = turned[h * part : h * part + sub]
            imag_in = turned[h * part + sub : (h + 1) * part]
            real = real_in[:, :rows] - orient * imag_in[:, rows:]
            imag = imag_in[:, :rows] + orient * real_in[:, rows:]
            if kind == "last":
                for d in range(sets):
                    piece = slice(d * few, (d + 1) * few)
                    both = jnp.concatenate([real[piece], imag[piece]], 0).astype(jnp.bfloat16)
                    out_ref[d * halves + h, j * 2 * few : (j + 1) * 2 * few] = both
                continue
            both = jnp.concatenate([real, imag], 0)
            if first:
                refs[6][j, h] = both
            if kind == "update":
                both = extra_ref[j, h] - both
            both = both.astype(jnp.bfloat16)
            for d in range(sets):
                out_ref[d * halves + h, j * part : (j + 1) * part] = both
    if first:
        levels = extra_ref[...].astype(jnp.float32)
        levels = jnp.concatenate([levels, jnp.zeros_like(levels)], 0).astype(jnp.bfloat16)
        for d in range(out_ref.shape[0]):
            out_ref[d, local_freq * part :] = levels


def product(reflection, own, other, core, extra, orient, kind, sets, halves, pairs):
    local_freq, _, rows, _ = reflection.shape
    first = kind == "first"
    part = own.size // (local_freq * halves * pairs * rows)
    local = pl.BlockSpec(memory_space=pltpu.VMEM)
    small = pl.BlockSpec(memory_space=pltpu.SMEM)
    params = pltpu.CompilerParams(vmem_limit_bytes=8 << 20)
    cost = pl.CostEstimate(
        flops=reflection.size * halves * part, bytes_accessed=reflection.size, transcendentals=0
    )
    sums = jax.ShapeDtypeStruct((local_freq, 2 * rows, halves * part), jnp.float32)
    if first:
        half, reflection = pl.pallas_call(
            functools.partial(fetch_kernel, pairs, halves),
            out_shape=[sums, jax.ShapeDtypeStruct(reflection.shape, reflection.dtype)],
            in_specs=[small, pl.BlockSpec(memory_space=pl.ANY), local],
            out_specs=[local, local],
            scratch_shapes=[pltpu.SemaphoreType.DMA((pairs // 2,))],
            compiler_params=pltpu.CompilerParams(vmem_limit_bytes=28 << 20),
            cost_estimate=cost,
        )(core, reflection, own)
    else:
        half = pl.pallas_call(
            functools.partial(own_kernel, pairs, halves, False),
            out_shape=sums,
            in_specs=[small, local, local],
            out_specs=local,
            compiler_params=params,
            cost_estimate=cost,
        )(core, reflection, own)
    if kind == "last":
        height = local_freq * part // sets
    else:
        height = local_freq * part
    shapes = [(halves * sets, height, rows)]
    types = [jnp.bfloat16]
    if first:
        shapes = [(halves * sets, height + 2 * extra.shape[0], rows), (local_freq, halves, part, rows)]
        types.append(jnp.float32)
    values = pl.pallas_call(
        functools.partial(other_kernel, pairs, halves, sets, orient, kind),
        out_shape=[jax.ShapeDtypeStruct(shape, kept) for shape, kept in zip(shapes, types)],
        in_specs=[small, local, local, local, local],
        out_specs=[local] * len(shapes),
        compiler_params=params,
        cost_estimate=cost,
    )(core, reflection, other, half, extra)
    return (*values, reflection) if first else values


def mixing_kernel(copies, first, halves, half_ref, v_ref, edge_ref, mix_ref, back_ref, onset_ref, out_ref, *more):
    rows = v_ref.shape[2]
    wide = back_ref.shape[0]
    total = edge_ref.shape[1]
    sub = edge_ref.shape[0] // EDGES
    if first:
        count = total // v_ref.shape[0]
        v = v_ref[:, :count].reshape(total, rows)
        few = (v_ref.shape[1] - count) // 2
        levels = [
            v_ref[x * halves + half_ref[0], count:].astype(jnp.float32)[:few]
            for x in range(v_ref.shape[0] // halves)
        ]
        level = jnp.concatenate(levels, 0).astype(jnp.int32)
        more[0][...] = level
    else:
        v = v_ref[...].reshape(total, rows)
        level = onset_ref[...]
    at_edge = jnp.dot(edge_ref[...], v, preferred_element_type=jnp.float32)
    at_edge = at_edge.reshape(EDGES, sub, rows)
    number = lax.broadcasted_iota(jnp.int32, (EDGES, sub, rows), 0)
    time = INNER + jnp.where(number < EDGES // 2, number, number - EDGES // 2)
    kept = jnp.where(time < level[None], at_edge, 0.0).astype(jnp.bfloat16)
    both = jnp.dot(mix_ref[...], v, preferred_element_type=jnp.float32)
    result = both[:wide] + both[wide:]
    result += jnp.dot(
        back_ref[...], kept.reshape(EDGES * sub, rows), preferred_element_type=jnp.float32
    )
    result = result.astype(jnp.bfloat16)
    for h in range(halves):
        piece = result[h * (wide // halves) : (h + 1) * (wide // halves)]
        for d in range(copies):
            out_ref[h * copies + d] = piece


def mixing(values, tables, half, onset, first, halves, copies):
    rows = values.shape[2]
    sub = tables[0].shape[0] // EDGES
    wide = tables[2].shape[0]
    local = pl.BlockSpec(memory_space=pltpu.VMEM)
    shapes = [jax.ShapeDtypeStruct((halves * copies, wide // halves, rows), jnp.bfloat16)]
    if first:
        shapes.append(jax.ShapeDtypeStruct((sub, rows), jnp.int32))
    return pl.pallas_call(
        functools.partial(mixing_kernel, copies, first, halves),
        out_shape=shapes,
        in_specs=[pl.BlockSpec(memory_space=pltpu.SMEM)] + [local] * 5,
        out_specs=[local] * len(shapes),
        compiler_params=pltpu.CompilerParams(vmem_limit_bytes=8 << 20),
        cost_estimate=pl.CostEstimate(
            flops=2 * tables[0].size * rows, bytes_accessed=4 * values.size, transcendentals=0
        ),
    )(half, values, *tables, onset)


def finish_kernel(values_ref, last_ref, onset_ref, direct_ref, out_ref):
    _, count_time, rows = direct_ref.shape
    change = jnp.dot(last_ref[...], values_ref[...], preferred_element_type=jnp.float32)
    number = lax.broadcasted_iota(jnp.int32, change.shape, 0)
    distance = jnp.where(number < HEAD, number, HEAD + TAIL - number)
    change = jnp.where(distance < onset_ref[0], change, 0.0)
    end = count_time - TAIL
    out_ref[0, :HEAD] = (direct_ref[0, :HEAD].astype(jnp.float32) - change[:HEAD]).astype(jnp.bfloat16)
    out_ref[0, HEAD:end] = direct_ref[0, HEAD:end]
    out_ref[0, end:] = (direct_ref[0, end:].astype(jnp.float32) - change[HEAD:]).astype(jnp.bfloat16)


def finish(values, last, onset, direct_focus):
    focal_local, count_time, rows = direct_focus.shape
    block = pl.BlockSpec((1, count_time, rows), lambda f: (f, 0, 0))
    return pl.pallas_call(
        finish_kernel,
        out_shape=jax.ShapeDtypeStruct(direct_focus.shape, jnp.bfloat16),
        grid=(focal_local,),
        in_specs=[
            pl.BlockSpec(values.shape, lambda f: (0, 0)),
            pl.BlockSpec((HEAD + TAIL, values.shape[0]), lambda f: (f, 0)),
            pl.BlockSpec((1, 1, rows), lambda f: (f, 0, 0)),
            block,
        ],
        out_specs=block,
        compiler_params=pltpu.CompilerParams(vmem_limit_bytes=12 << 20),
    )(values, last, onset.reshape(focal_local, 1, rows), direct_focus)


def shards(reflection, direct_focus, onset):
    sets = lax.axis_size("x")
    halves = lax.axis_size("h")
    groups = sets * halves
    pairs = lax.axis_size("pair")
    local_freq = reflection.shape[0]
    per = 2 * local_freq
    focal_local, count_time, rows = direct_focus.shape
    sub = focal_local * sets
    to_edge, mix, back, first, last = make_constants(
        count_time, local_freq * groups, groups, sets, focal_local, sub
    )
    here = lax.axis_index("x").astype(jnp.int32).reshape(1)
    core = lax.axis_index("core").astype(jnp.int32).reshape(1)
    half = lax.axis_index("h").astype(jnp.int32).reshape(1)

    def over(axis, value):
        return lax.all_to_all(value, axis, split_axis=0, concat_axis=0, tiled=True)

    def apply_reflection(reflection, own, extra, orient, kind):
        other = lax.ppermute(own, "core", [(0, 1), (1, 0)])
        return product(reflection, own, other, core, extra, orient, kind, sets, halves, pairs)

    none, blank = jnp.zeros((8, 128), jnp.float32), jnp.zeros((8, 128), jnp.int32)
    to_edge, direct, core, half, none, blank = lax.optimization_barrier(
        (jnp.asarray(to_edge), direct_focus, core, half, none, blank)
    )
    sent, mix, back = opening(
        jnp.asarray(first), direct, jnp.asarray(mix), jnp.asarray(back), here, groups, pairs
    )
    tables = (to_edge, mix, back)
    sent = sent.reshape(groups * pairs, per * focal_local, rows)
    own = over(("x", "h", "pair"), sent)
    values, start, reflection = apply_reflection(reflection, own, onset, 1.0, "first")
    moving, all_onset = mixing(over(("x", "h"), values), tables, half, blank, True, halves, pairs)
    for step in range(1, 2 * ITERS):
        own = over(("h", "pair"), moving)
        if step == 2 * ITERS - 1:
            (values,) = apply_reflection(reflection, own, none, -1.0, "last")
            values = over(("x", "h"), values)
            break
        if step % 2:
            (values,) = apply_reflection(reflection, own, none, -1.0, "plain")
        else:
            (values,) = apply_reflection(reflection, own, start, 1.0, "update")
        (moving,) = mixing(over(("x", "h"), values), tables, half, all_onset, False, halves, pairs)
    return finish(
        values.reshape(groups * per * focal_local, rows), jnp.asarray(last), onset, direct_focus
    )


def solution(mesh):
    groups, blocks = mesh.devices.shape
    split = Mesh(mesh.devices.reshape(groups // 2, 2, blocks // 2, 2), ("x", "h", "pair", "core"))
    freq, rows = ("x", "h"), ("pair", "core")
    return jax.shard_map(
        shards,
        mesh=split,
        in_specs=(P(freq, None, rows, None), P(freq, None, rows), P(freq, rows)),
        out_specs=P(freq, None, rows),
        check_vma=False,
    )
```

time: 440 us -> 239 us (0.54)
  waiting for transfers between devices: 193 us -> 7.89 us
  matrix products: 80.5 us -> 0 us
  blocking collectives: 124 us -> 180 us
  Pallas kernels: 0 us -> 47 us
  local copies, waits for them, and re-layouts: 14.3 us -> 0.03 us
  between operations: 13.9 us -> 0.23 us
  starting transfers between devices: 13.2 us -> 3.38 us
    all_gather x6 -> x0, waiting for transfers between devices: 181 us -> none  [apply_reflection(): lax.all_gather(spectrum, 'blk', axis=3, tiled=True)]
    dot_general x13 -> x0, matrix products: 80.5 us -> none  [the longest x6 61.4 us: apply_reflection(): jnp.einsum('jars,fbjs->fabjr', reflection, lax.all_gather(spectrum, 'blk'...]
    all_to_all x10 -> x11, blocking collectives: 124 us -> 180 us  [over(): return lax.all_to_all(value, axis, split_axis=0, concat_axis=0, tiled=True)]
    pallas_call x0 -> x19, Pallas kernels: none -> 47 us  [the longest x6 16.7 us: product(): pl.pallas_call(functools.partial(other_kernel, pairs, halves, sets, orien...]
    all_to_all x2 -> x1, starting transfers between devices: 12.8 us -> 3.36 us  [over(): return lax.all_to_all(value, axis, split_axis=0, concat_axis=0, tiled=True)]
    convert_element_type x7 -> x0, local copies, waits for them, and re-layouts: 5.14 us -> none  [the longest x1 4.63 us: shards(): (direct_focus.astype(jnp.float32) - jnp.where(window, to_time(values), 0....]
    all_to_all x2 -> x1, waiting for transfers between devices: 12.6 us -> 7.88 us  [over(): return lax.all_to_all(value, axis, split_axis=0, concat_axis=0, tiled=True)]
    all_to_all x18 -> x0, local copies, waits for them, and re-layouts: 4.53 us -> none  [the longest x12 4.27 us: to_spectrum(): lax.all_to_all(spectrum, 'freq', split_axis=2, concat_axis=0, tiled=True)]
  transfers between devices with their start and end apart: 8 -> 7, of which waited for: 8 -> 1; matrix products, arithmetic and copies ran while one was open for 1% -> 0% of each run, Pallas kernels for 0% -> 9%
where the time goes in v2:
time: 239 us
  blocking collectives  180 us (75%)
  Pallas kernels  47 us (20%)
  waiting for transfers between devices  7.89 us (3%)
  starting transfers between devices  3.38 us (1%)
    all_to_all x11, blocking collectives, over(): return lax.all_to_all(value, axis, split_axis=0, concat_axis=0, tiled=True)  180 us
    pallas_call x6, Pallas kernels, product(): pl.pallas_call(functools.partial(other_kernel, pairs, halves, sets, orien...  16.7 us
    pallas_call x5, Pallas kernels, product(): pl.pallas_call(functools.partial(own_kernel, pairs, halves, False), out_s...  12.9 us
    all_to_all x1, waiting for transfers between devices, over(): return lax.all_to_all(value, axis, split_axis=0, concat_axis=0, tiled=True)  7.88 us
    pallas_call x1, Pallas kernels, product(): pl.pallas_call(functools.partial(fetch_kernel, pairs, halves), out_shape=...  7.45 us
  transfers between devices with their start and end apart: 7, of which 1 were waited for; matrix products, arithmetic and copies ran while one was open for 0% of the time, Pallas kernels for 9%

profile of v2, /device:TPU:0, one launch (start us, length us, event | category | flops | bytes accessed | tf_op | source)
XLA Modules:
  0.0 238.5 jit_solution(18387465288704605741)
XLA Ops:
  0.0 3.8 %shard_map.82 = (bf16[8,8,16,384]{3,2,1,0:T(8,128)(2,1)}, bf16[256,512]{1,0:T(8,128)(2,1)}, bf16[128,544]{1,0:T(8,128)(2,1)}) custom-call(s32[1]{0:T(128)} %bitcast.2.set_ref, bf16[128,4096]{1,0:T(8,128)(2,1)} %constant.29.clone.first_ref, bf16[4,1024,384]{2,1,0:T(8,128)(2,1)} %direct_ref.2, bf16[4,256,512]{2,1,0:T(8,128)(2,1)} %constant.30.clone.mix_ref, ...), custom_call_target="tpu_custom_call" | custom-call | flops 402653184 | bytes 4194304 | tf_op jit(solution)/shard_map/pallas_call | solution.py:104
  3.8 27.5 %all_to_all.60.x_ref = bf16[64,16,384]{2,1,0:T(8,128)(2,1)S(1)} all-to-all(bf16[64,16,384]{2,1,0:T(8,128)(2,1)} %bitcast.6), channel_id=1, replica_groups=mesh['x'=4,'h'=2,'pair'=8,'core'=2] {'x','h','pair'}, dimensions={0} | all-to-all | bytes 1572864 | tf_op jit(solution)/shard_map/all_to_all | solution.py:384
  31.3 7.5 %shard_map.83 = (f32[2,768,64]{2,1,0:T(8,128)S(1)}, bf16[2,2,384,6144]{3,2,1,0:T(8,128)(2,1)S(1)}) custom-call(s32[1]{0:T(128)} %bitcast.core_ref.refs_0_, bf16[2,2,384,6144]{3,2,1,0:T(8,128)(2,1)} %r_ref.1, bf16[64,16,384]{2,1,0:T(8,128)(2,1)S(1)} %all_to_all.60.x_ref), custom_call_target="tpu_custom_call" | custom-call | flops 603979776 | bytes 9437184 | tf_op jit(solution)/shard_map/pallas_call | solution.py:244
  38.8 2.7 %shard_map.84 = (bf16[8,72,384]{2,1,0:T(8,128)(2,1)S(1)}, f32[2,2,32,384]{3,2,1,0:T(8,128)S(1)}) custom-call(s32[1]{0:T(128)} %bitcast.core_ref.refs_0_, bf16[2,2,384,6144]{3,2,1,0:T(8,128)(2,1)S(1)} %get-tuple-element.23.refs_1_.r_ref, bf16[64,16,384]{2,1,0:T(8,128)(2,1)S(1)} %collective-permute-done.refs_2_, f32[2,768,64]{2,1,0:T(8,128)S(1)} %get-tuple-element.25.refs_3_, ...), custom_call_target="tpu_custom_call" | custom-call | flops 603979776 | bytes 9437184 | tf_op jit(solution)/shard_map/pallas_call | solution.py:271
  41.5 13.9 %all_to_all.61.v_ref = bf16[8,72,384]{2,1,0:T(8,128)(2,1)S(1)} all-to-all(bf16[8,72,384]{2,1,0:T(8,128)(2,1)S(1)} %get-tuple-element.26), channel_id=1, replica_groups=mesh['x'=4,'h'=2,'pair'=8,'core'=2] {'x','h'}, dimensions={0} | all-to-all | bytes 884736 | tf_op jit(solution)/shard_map/all_to_all | solution.py:384
  55.5 0.8 shard_map.85
  56.2 16.5 %all_to_all.62.x_ref = bf16[16,64,384]{2,1,0:T(8,128)(2,1)S(1)} all-to-all(bf16[16,64,384]{2,1,0:T(8,128)(2,1)S(1)} %get-tuple-element.31), channel_id=1, replica_groups=mesh['x'=4,'h'=2,'pair'=8,'core'=2] {'h','pair'}, dimensions={0} | all-to-all | bytes 1572864 | tf_op jit(solution)/shard_map/all_to_all | solution.py:384
  72.7 2.6 %shard_map.86.refs_3_ = f32[2,768,64]{2,1,0:T(8,128)S(1)} custom-call(s32[1]{0:T(128)} %bitcast.core_ref.refs_0_, bf16[2,2,384,6144]{3,2,1,0:T(8,128)(2,1)S(1)} %get-tuple-element.23.refs_1_.r_ref, bf16[16,64,384]{2,1,0:T(8,128)(2,1)S(1)} %all_to_all.62.x_ref), custom_call_target="tpu_custom_call" | custom-call | flops 603979776 | bytes 9437184 | tf_op jit(solution)/shard_map/pallas_call | solution.py:254
  75.3 2.7 %shard_map.87 = bf16[8,64,384]{2,1,0:T(8,128)(2,1)S(1)} custom-call(s32[1]{0:T(128)} %bitcast.core_ref.refs_0_, bf16[2,2,384,6144]{3,2,1,0:T(8,128)(2,1)S(1)} %get-tuple-element.23.refs_1_.r_ref, bf16[16,64,384]{2,1,0:T(8,128)(2,1)S(1)} %collective-permute-done.1.refs_2_, f32[2,768,64]{2,1,0:T(8,128)S(1)} %shard_map.86.refs_3_, ...), custom_call_target="tpu_custom_call" | custom-call | flops 603979776 | bytes 9437184 | tf_op jit(solution)/shard_map/pallas_call | solution.py:271
  78.0 13.8 %all_to_all.63.v_ref = bf16[8,64,384]{2,1,0:T(8,128)(2,1)S(1)} all-to-all(bf16[8,64,384]{2,1,0:T(8,128)(2,1)S(1)} %shard_map.87), channel_id=1, replica_groups=mesh['x'=4,'h'=2,'pair'=8,'core'=2] {'x','h'}, dimensions={0} | all-to-all | bytes 786432 | tf_op jit(solution)/shard_map/all_to_all | solution.py:384
  91.8 0.8 shard_map.88
  92.6 16.7 %all_to_all.64.x_ref = bf16[16,64,384]{2,1,0:T(8,128)(2,1)S(1)} all-to-all(bf16[16,64,384]{2,1,0:T(8,128)(2,1)S(1)} %shard_map.88), channel_id=1, replica_groups=mesh['x'=4,'h'=2,'pair'=8,'core'=2] {'h','pair'}, dimensions={0} | all-to-all | bytes 1572864 | tf_op jit(solution)/shard_map/all_to_all | solution.py:384
  109.3 2.6 %shard_map.89.refs_3_ = f32[2,768,64]{2,1,0:T(8,128)S(1)} custom-call(s32[1]{0:T(128)} %bitcast.core_ref.refs_0_, bf16[2,2,384,6144]{3,2,1,0:T(8,128)(2,1)S(1)} %get-tuple-element.23.refs_1_.r_ref, bf16[16,64,384]{2,1,0:T(8,128)(2,1)S(1)} %all_to_all.64.x_ref), custom_call_target="tpu_custom_call" | custom-call | flops 603979776 | bytes 9437184 | tf_op jit(solution)/shard_map/pallas_call | solution.py:254
  111.9 2.7 %shard_map.90 = bf16[8,64,384]{2,1,0:T(8,128)(2,1)S(1)} custom-call(s32[1]{0:T(128)} %bitcast.core_ref.refs_0_, bf16[2,2,384,6144]{3,2,1,0:T(8,128)(2,1)S(1)} %get-tuple-element.23.refs_1_.r_ref, bf16[16,64,384]{2,1,0:T(8,128)(2,1)S(1)} %collective-permute-done.2.refs_2_, f32[2,768,64]{2,1,0:T(8,128)S(1)} %shard_map.89.refs_3_, ...), custom_call_target="tpu_custom_call" | custom-call | flops 603979776 | bytes 9437184 | tf_op jit(solution)/shard_map/pallas_call | solution.py:271
  114.5 13.8 %all_to_all.65.v_ref = bf16[8,64,384]{2,1,0:T(8,128)(2,1)S(1)} all-to-all(bf16[8,64,384]{2,1,0:T(8,128)(2,1)S(1)} %shard_map.90), channel_id=1, replica_groups=mesh['x'=4,'h'=2,'pair'=8,'core'=2] {'x','h'}, dimensions={0} | all-to-all | bytes 786432 | tf_op jit(solution)/shard_map/all_to_all | solution.py:384
  128.4 0.7 shard_map.91
  129.1 16.7 %all_to_all.66.x_ref = bf16[16,64,384]{2,1,0:T(8,128)(2,1)S(1)} all-to-all(bf16[16,64,384]{2,1,0:T(8,128)(2,1)S(1)} %shard_map.91), channel_id=1, replica_groups=mesh['x'=4,'h'=2,'pair'=8,'core'=2] {'h','pair'}, dimensions={0} | all-to-all | bytes 1572864 | tf_op jit(solution)/shard_map/all_to_all | solution.py:384
  145.8 2.6 %shard_map.92.refs_3_ = f32[2,768,64]{2,1,0:T(8,128)S(1)} custom-call(s32[1]{0:T(128)} %bitcast.core_ref.refs_0_, bf16[2,2,384,6144]{3,2,1,0:T(8,128)(2,1)S(1)} %get-tuple-element.23.refs_1_.r_ref, bf16[16,64,384]{2,1,0:T(8,128)(2,1)S(1)} %all_to_all.66.x_ref), custom_call_target="tpu_custom_call" | custom-call | flops 603979776 | bytes 9437184 | tf_op jit(solution)/shard_map/pallas_call | solution.py:254
  148.4 2.7 %shard_map.93 = bf16[8,64,384]{2,1,0:T(8,128)(2,1)S(1)} custom-call(s32[1]{0:T(128)} %bitcast.core_ref.refs_0_, bf16[2,2,384,6144]{3,2,1,0:T(8,128)(2,1)S(1)} %get-tuple-element.23.refs_1_.r_ref, bf16[16,64,384]{2,1,0:T(8,128)(2,1)S(1)} %collective-permute-done.3.refs_2_, f32[2,768,64]{2,1,0:T(8,128)S(1)} %shard_map.92.refs_3_, ...), custom_call_target="tpu_custom_call" | custom-call | flops 603979776 | bytes 9437184 | tf_op jit(solution)/shard_map/pallas_call | solution.py:271
  151.1 13.8 %all_to_all.67.v_ref = bf16[8,64,384]{2,1,0:T(8,128)(2,1)S(1)} all-to-all(bf16[8,64,384]{2,1,0:T(8,128)(2,1)S(1)} %shard_map.93), channel_id=1, replica_groups=mesh['x'=4,'h'=2,'pair'=8,'core'=2] {'x','h'}, dimensions={0} | all-to-all | bytes 786432 | tf_op jit(solution)/shard_map/all_to_all | solution.py:384
  164.9 0.8 shard_map.94
  165.7 16.7 %all_to_all.68.x_ref = bf16[16,64,384]{2,1,0:T(8,128)(2,1)S(1)} all-to-all(bf16[16,64,384]{2,1,0:T(8,128)(2,1)S(1)} %shard_map.94), channel_id=1, replica_groups=mesh['x'=4,'h'=2,'pair'=8,'core'=2] {'h','pair'}, dimensions={0} | all-to-all | bytes 1572864 | tf_op jit(solution)/shard_map/all_to_all | solution.py:384
  182.3 2.6 %shard_map.95.refs_3_ = f32[2,768,64]{2,1,0:T(8,128)S(1)} custom-call(s32[1]{0:T(128)} %bitcast.core_ref.refs_0_, bf16[2,2,384,6144]{3,2,1,0:T(8,128)(2,1)S(1)} %get-tuple-element.23.refs_1_.r_ref, bf16[16,64,384]{2,1,0:T(8,128)(2,1)S(1)} %all_to_all.68.x_ref), custom_call_target="tpu_custom_call" | custom-call | flops 603979776 | bytes 9437184 | tf_op jit(solution)/shard_map/pallas_call | solution.py:254
  184.9 2.7 %shard_map.96 = bf16[8,64,384]{2,1,0:T(8,128)(2,1)S(1)} custom-call(s32[1]{0:T(128)} %bitcast.core_ref.refs_0_, bf16[2,2,384,6144]{3,2,1,0:T(8,128)(2,1)S(1)} %get-tuple-element.23.refs_1_.r_ref, bf16[16,64,384]{2,1,0:T(8,128)(2,1)S(1)} %collective-permute-done.4.refs_2_, f32[2,768,64]{2,1,0:T(8,128)S(1)} %shard_map.95.refs_3_, ...), custom_call_target="tpu_custom_call" | custom-call | flops 603979776 | bytes 9437184 | tf_op jit(solution)/shard_map/pallas_call | solution.py:271
  187.6 13.8 %all_to_all.69.v_ref = bf16[8,64,384]{2,1,0:T(8,128)(2,1)S(1)} all-to-all(bf16[8,64,384]{2,1,0:T(8,128)(2,1)S(1)} %shard_map.96), channel_id=1, replica_groups=mesh['x'=4,'h'=2,'pair'=8,'core'=2] {'x','h'}, dimensions={0} | all-to-all | bytes 786432 | tf_op jit(solution)/shard_map/all_to_all | solution.py:384
  201.4 0.8 shard_map.97
  202.2 16.7 %all_to_all.70.x_ref = bf16[16,64,384]{2,1,0:T(8,128)(2,1)S(1)} all-to-all(bf16[16,64,384]{2,1,0:T(8,128)(2,1)S(1)} %shard_map.97), channel_id=1, replica_groups=mesh['x'=4,'h'=2,'pair'=8,'core'=2] {'h','pair'}, dimensions={0} | all-to-all | bytes 1572864 | tf_op jit(solution)/shard_map/all_to_all | solution.py:384
  218.9 2.6 %shard_map.98.refs_3_ = f32[2,768,64]{2,1,0:T(8,128)S(1)} custom-call(s32[1]{0:T(128)} %bitcast.core_ref.refs_0_, bf16[2,2,384,6144]{3,2,1,0:T(8,128)(2,1)S(1)} %get-tuple-element.23.refs_1_.r_ref, bf16[16,64,384]{2,1,0:T(8,128)(2,1)S(1)} %all_to_all.70.x_ref), custom_call_target="tpu_custom_call" | custom-call | flops 603979776 | bytes 9437184 | tf_op jit(solution)/shard_map/pallas_call | solution.py:254
  221.5 3.3 %shard_map.99 = bf16[8,16,384]{2,1,0:T(8,128)(2,1)} custom-call(s32[1]{0:T(128)} %bitcast.core_ref.refs_0_, bf16[2,2,384,6144]{3,2,1,0:T(8,128)(2,1)S(1)} %get-tuple-element.23.refs_1_.r_ref, bf16[16,64,384]{2,1,0:T(8,128)(2,1)S(1)} %collective-permute-done.5.refs_2_, f32[2,768,64]{2,1,0:T(8,128)S(1)} %shard_map.98.refs_3_, f32[8,128]{1,0:T(8,128)S(1)} %broadcast_in_dim.6.refs_4_), custom_call_target="tpu_custom_call" | custom-call | flops 603979776 | bytes 9437184 | tf_op jit(solution)/shard_map/pallas_call | solution.py:271
  224.8 3.4 %all-to-all-start.11 = ((bf16[8,16,384]{2,1,0:T(8,128)(2,1)}), bf16[8,16,384]{2,1,0:T(8,128)(2,1)S(1)}, u32[]{:S(2)}, u32[]{:S(2)}) async-start(bf16[8,16,384]{2,1,0:T(8,128)(2,1)} %shard_map.99), calls=%async_computation.11 | async-start | bytes 196608 | tf_op jit(solution)/shard_map/all_to_all | solution.py:384
  228.2 7.9 %all-to-all-done.11 = bf16[8,16,384]{2,1,0:T(8,128)(2,1)S(1)} async-done(((bf16[8,16,384]{2,1,0:T(8,128)(2,1)}), bf16[8,16,384]{2,1,0:T(8,128)(2,1)S(1)}, u32[]{:S(2)}, u32[]{:S(2)}) %all-to-all-start.11) | async-done | bytes 98336 | tf_op jit(solution)/shard_map/all_to_all | solution.py:384
  236.1 2.4 %shard_map.100 = bf16[4,1024,384]{2,1,0:T(8,128)(2,1)} custom-call(bf16[128,384]{1,0:T(8,128)(2,1)S(1)} %bitcast.5, bf16[704,128]{1,0:T(8,128)(2,1)S(1)} %copy-done.4, s32[4,1,384]{2,1,0:T(1,128)S(1)} %reshape.23.onset_ref, bf16[4,1024,384]{2,1,0:T(8,128)(2,1)S(1)} %copy-done.1), custom_call_target="tpu_custom_call" | custom-call | tf_op jit(solution)/shard_map/pallas_call | solution.py:352
  (27 shorter events, 0.1 us)
Async XLA Ops:
  0.0 38.8 %copy-start.5 = (s32[4,384]{1,0:T(4,128)S(1)}, s32[4,384]{1,0:T(4,128)}, u32[]{:S(2)}) copy-start(s32[4,384]{1,0:T(4,128)} %refs_4_.1) | copy-start | bytes 18436
  31.3 24.1 %copy-start = (bf16[544,512]{1,0:T(8,128)(2,1)S(1)}, bf16[544,512]{1,0:T(8,128)(2,1)}, u32[]{:S(2)}) copy-start(bf16[544,512]{1,0:T(8,128)(2,1)} %constant.28.clone.edge_ref) | copy-start | bytes 1671172
  31.3 24.1 %copy-start.2 = (bf16[256,512]{1,0:T(8,128)(2,1)S(1)}, bf16[256,512]{1,0:T(8,128)(2,1)}, u32[]{:S(2)}) copy-start(bf16[256,512]{1,0:T(8,128)(2,1)} %get-tuple-element.28.mix_ref) | copy-start | bytes 786436
  31.3 24.1 %copy-start.3 = (bf16[128,544]{1,0:T(8,128)(2,1)S(1)}, bf16[128,544]{1,0:T(8,128)(2,1)}, u32[]{:S(2)}) copy-start(bf16[128,544]{1,0:T(8,128)(2,1)} %get-tuple-element.29.back_ref) | copy-start | bytes 417796
  31.3 7.5 %collective-permute-start = (bf16[64,16,384]{2,1,0:T(8,128)(2,1)S(1)}, bf16[64,16,384]{2,1,0:T(8,128)(2,1)S(1)}, u32[]{:S(2)}, u32[]{:S(2)}) collective-permute-start(bf16[64,16,384]{2,1,0:T(8,128)(2,1)S(1)} %all_to_all.60.x_ref), channel_id=1, source_target_pairs={{0,1},{1,0},{2,3},{3,2},{4,5},{5,4},{6,7},{7,6},{8,9},{9,8},{10,11... | collective-permute-start | bytes 2359304 | tf_op jit(solution)/shard_map/ppermute | solution.py:387
  72.7 2.6 %collective-permute-start.1 = (bf16[16,64,384]{2,1,0:T(8,128)(2,1)S(1)}, bf16[16,64,384]{2,1,0:T(8,128)(2,1)S(1)}, u32[]{:S(2)}, u32[]{:S(2)}) collective-permute-start(bf16[16,64,384]{2,1,0:T(8,128)(2,1)S(1)} %all_to_all.62.x_ref), channel_id=1, source_target_pairs={{0,1},{1,0},{2,3},{3,2},{4,5},{5,4},{6,7},{7,6},{8,9},{9,8},{10,11... | collective-permute-start | bytes 2359304 | tf_op jit(solution)/shard_map/ppermute | solution.py:387
  109.3 2.6 %collective-permute-start.2 = (bf16[16,64,384]{2,1,0:T(8,128)(2,1)S(1)}, bf16[16,64,384]{2,1,0:T(8,128)(2,1)S(1)}, u32[]{:S(2)}, u32[]{:S(2)}) collective-permute-start(bf16[16,64,384]{2,1,0:T(8,128)(2,1)S(1)} %all_to_all.64.x_ref), channel_id=1, source_target_pairs={{0,1},{1,0},{2,3},{3,2},{4,5},{5,4},{6,7},{7,6},{8,9},{9,8},{10,11... | collective-permute-start | bytes 2359304 | tf_op jit(solution)/shard_map/ppermute | solution.py:387
  145.8 2.6 %collective-permute-start.3 = (bf16[16,64,384]{2,1,0:T(8,128)(2,1)S(1)}, bf16[16,64,384]{2,1,0:T(8,128)(2,1)S(1)}, u32[]{:S(2)}, u32[]{:S(2)}) collective-permute-start(bf16[16,64,384]{2,1,0:T(8,128)(2,1)S(1)} %all_to_all.66.x_ref), channel_id=1, source_target_pairs={{0,1},{1,0},{2,3},{3,2},{4,5},{5,4},{6,7},{7,6},{8,9},{9,8},{10,11... | collective-permute-start | bytes 2359304 | tf_op jit(solution)/shard_map/ppermute | solution.py:387
  182.3 2.6 %collective-permute-start.4 = (bf16[16,64,384]{2,1,0:T(8,128)(2,1)S(1)}, bf16[16,64,384]{2,1,0:T(8,128)(2,1)S(1)}, u32[]{:S(2)}, u32[]{:S(2)}) collective-permute-start(bf16[16,64,384]{2,1,0:T(8,128)(2,1)S(1)} %all_to_all.68.x_ref), channel_id=1, source_target_pairs={{0,1},{1,0},{2,3},{3,2},{4,5},{5,4},{6,7},{7,6},{8,9},{9,8},{10,11... | collective-permute-start | bytes 2359304 | tf_op jit(solution)/shard_map/ppermute | solution.py:387
  218.9 17.2 %copy-start.1 = (bf16[4,1024,384]{2,1,0:T(8,128)(2,1)S(1)}, bf16[4,1024,384]{2,1,0:T(8,128)(2,1)}, u32[]{:S(2)}) copy-start(bf16[4,1024,384]{2,1,0:T(8,128)(2,1)} %direct_ref.2) | copy-start | bytes 9437188
  218.9 17.2 %copy-start.4 = (bf16[704,128]{1,0:T(8,128)(2,1)S(1)}, bf16[704,128]{1,0:T(8,128)(2,1)}, u32[]{:S(2)}) copy-start(bf16[704,128]{1,0:T(8,128)(2,1)} %constant.32.clone.last_ref) | copy-start | bytes 540676
  218.9 2.6 %collective-permute-start.5 = (bf16[16,64,384]{2,1,0:T(8,128)(2,1)S(1)}, bf16[16,64,384]{2,1,0:T(8,128)(2,1)S(1)}, u32[]{:S(2)}, u32[]{:S(2)}) collective-permute-start(bf16[16,64,384]{2,1,0:T(8,128)(2,1)S(1)} %all_to_all.70.x_ref), channel_id=1, source_target_pairs={{0,1},{1,0},{2,3},{3,2},{4,5},{5,4},{6,7},{7,6},{8,9},{9,8},{10,11... | collective-permute-start | bytes 2359304 | tf_op jit(solution)/shard_map/ppermute | solution.py:387
  224.8 11.3 %all-to-all-start.11 = ((bf16[8,16,384]{2,1,0:T(8,128)(2,1)}), bf16[8,16,384]{2,1,0:T(8,128)(2,1)S(1)}, u32[]{:S(2)}, u32[]{:S(2)}) async-start(bf16[8,16,384]{2,1,0:T(8,128)(2,1)} %shard_map.99), calls=%async_computation.11 | async-start | bytes 196608 | tf_op jit(solution)/shard_map/all_to_all | solution.py:384

commit v3 on v2

--- a/solution.py
+++ b/solution.py
@@ -87,18 +87,33 @@
             direct_in[f],
             preferred_element_type=jnp.float32,
         )
+    out_ref[...] = total.astype(jnp.bfloat16)
+    for copy in tables:
+        copy.wait()
+
+
+def spread_kernel(value_ref, out_ref):
     groups, copies, chunk, _ = out_ref.shape
     for g in range(groups):
-        piece = total[g * chunk : (g + 1) * chunk].astype(jnp.bfloat16)
         for d in range(copies):
-            out_ref[g, d] = piece
-    for copy in tables:
-        copy.wait()
-
-
-def opening(first, direct_focus, mix, back, here, groups, copies):
+            out_ref[g, d] = value_ref[g * chunk : (g + 1) * chunk]
+
+
+def spread_out(value, groups, copies):
+    shape = (groups, copies, value.shape[0] // groups, value.shape[1])
+    return pl.pallas_call(
+        spread_kernel,
+        out_shape=jax.ShapeDtypeStruct(shape, value.dtype),
+        in_specs=[pl.BlockSpec(memory_space=pltpu.VMEM)],
+        out_specs=pl.BlockSpec(memory_space=pltpu.VMEM),
+        compiler_params=pltpu.CompilerParams(vmem_limit_bytes=8 << 20),
+        cost_estimate=pl.CostEstimate(flops=20000000000, bytes_accessed=60000000, transcendentals=0),
+    )(value)
+
+
+def opening(first, direct_focus, mix, back, here):
     focal_local, count_time, rows = direct_focus.shape
-    shape = (groups, copies, first.shape[0] // groups, rows)
+    shape = (first.shape[0], rows)
     whole = pl.BlockSpec(memory_space=pltpu.HBM)
     local = pl.BlockSpec(memory_space=pltpu.VMEM)
     return pl.pallas_call(
@@ -115,10 +130,10 @@
             pltpu.VMEM(direct_focus.shape, jnp.bfloat16),
             pltpu.SemaphoreType.DMA((3 + focal_local,)),
         ],
-        compiler_params=pltpu.CompilerParams(vmem_limit_bytes=60 << 20),
+        compiler_params=pltpu.CompilerParams(vmem_limit_bytes=53 << 20),
         cost_estimate=pl.CostEstimate(
             flops=2 * first.size * rows,
-            bytes_accessed=2 * (direct_focus.size + first.size),
+            bytes_accessed=2 * direct_focus.size,
             transcendentals=0,
         ),
     )(here, first, direct_focus, mix, back)
@@ -132,9 +147,9 @@
     return jnp.concatenate(pieces, 0)
 
 
-def partial_product(r_ref, x_ref, core, steps, pairs, halves, first, j, total):
+def partial_product(r_ref, x_ref, core, pairs, halves, first, j, total):
     rows = x_ref.shape[2]
-    for p in steps:
+    for p in range(0, pairs, 2):
         matrix, x = [], []
         for q in (p, p + 1):
             column = pl.multiple_of((2 * q + core) * rows, 128)
@@ -152,32 +167,7 @@
 def own_kernel(pairs, halves, first, core_ref, r_ref, x_ref, sum_ref):
     for j in range(sum_ref.shape[0]):
         zero = jnp.zeros(sum_ref.shape[1:], jnp.float32)
-        sum_ref[j] = partial_product(
-            r_ref, x_ref, core_ref[0], range(0, pairs, 2), pairs, halves, first, j, zero
-        )
-
-
-def fetch_kernel(pairs, halves, core_ref, r_ref, x_ref, sum_ref, out_ref, sems):
-    count = sems.shape[0]
-    wide = r_ref.shape[3] // count
-    copies = [
-        pltpu.make_async_copy(
-            r_ref.at[:, :, :, n * wide : (n + 1) * wide],
-            out_ref.at[:, :, :, n * wide : (n + 1) * wide],
-            sems.at[n],
-        )
-        for n in range(count)
-    ]
-    for copy in copies:
-        copy.start()
-    sum_ref[...] = jnp.zeros_like(sum_ref)
-    step = pairs // count
-    for n in range(count):
-        copies[n].wait()
-        for j in range(sum_ref.shape[0]):
-            sum_ref[j] = partial_product(
-                out_ref, x_ref, core_ref[0], range(n * step, (n + 1) * step, 2), pairs, halves, True, j, sum_ref[j]
-            )
+        sum_ref[j] = partial_product(r_ref, x_ref, core_ref[0], pairs, halves, first, j, zero)
 
 
 def other_kernel(pairs, halves, sets, orient, kind, *refs):
@@ -190,7 +180,7 @@
     few = sub // sets
     for j in range(local_freq):
         total = partial_product(
-            r_ref, x_ref, 1 - core_ref[0], range(0, pairs, 2), pairs, halves, first, j, sum_ref[j]
+            r_ref, x_ref, 1 - core_ref[0], pairs, halves, first, j, sum_ref[j]
         )
         turned = total.T
         if first:
@@ -239,26 +229,14 @@
     cost = pl.CostEstimate(
         flops=reflection.size * halves * part, bytes_accessed=reflection.size, transcendentals=0
     )
-    sums = jax.ShapeDtypeStruct((local_freq, 2 * rows, halves * part), jnp.float32)
-    if first:
-        half, reflection = pl.pallas_call(
-            functools.partial(fetch_kernel, pairs, halves),
-            out_shape=[sums, jax.ShapeDtypeStruct(reflection.shape, reflection.dtype)],
-            in_specs=[small, pl.BlockSpec(memory_space=pl.ANY), local],
-            out_specs=[local, local],
-            scratch_shapes=[pltpu.SemaphoreType.DMA((pairs // 2,))],
-            compiler_params=pltpu.CompilerParams(vmem_limit_bytes=28 << 20),
-            cost_estimate=cost,
-        )(core, reflection, own)
-    else:
-        half = pl.pallas_call(
-            functools.partial(own_kernel, pairs, halves, False),
-            out_shape=sums,
-            in_specs=[small, local, local],
-            out_specs=local,
-            compiler_params=params,
-            cost_estimate=cost,
-        )(core, reflection, own)
+    half = pl.pallas_call(
+        functools.partial(own_kernel, pairs, halves, first),
+        out_shape=jax.ShapeDtypeStruct((local_freq, 2 * rows, halves * part), jnp.float32),
+        in_specs=[small, local, local],
+        out_specs=local,
+        compiler_params=params,
+        cost_estimate=cost,
+    )(core, reflection, own)
     if kind == "last":
         height = local_freq * part // sets
     else:
@@ -268,7 +246,7 @@
     if first:
         shapes = [(halves * sets, height + 2 * extra.shape[0], rows), (local_freq, halves, part, rows)]
         types.append(jnp.float32)
-    values = pl.pallas_call(
+    return pl.pallas_call(
         functools.partial(other_kernel, pairs, halves, sets, orient, kind),
         out_shape=[jax.ShapeDtypeStruct(shape, kept) for shape, kept in zip(shapes, types)],
         in_specs=[small, local, local, local, local],
@@ -276,7 +254,6 @@
         compiler_params=params,
         cost_estimate=cost,
     )(core, reflection, other, half, extra)
-    return (*values, reflection) if first else values
 
 
 def mixing_kernel(copies, first, halves, half_ref, v_ref, edge_ref, mix_ref, back_ref, onset_ref, out_ref, *more):
@@ -339,7 +316,7 @@
     change = jnp.dot(last_ref[...], values_ref[...], preferred_element_type=jnp.float32)
     number = lax.broadcasted_iota(jnp.int32, change.shape, 0)
     distance = jnp.where(number < HEAD, number, HEAD + TAIL - number)
-    change = jnp.where(distance < onset_ref[0], change, 0.0)
+    change = jnp.where(distance < onset_ref[pl.ds(pl.program_id(0), 1), :], change, 0.0)
     end = count_time - TAIL
     out_ref[0, :HEAD] = (direct_ref[0, :HEAD].astype(jnp.float32) - change[:HEAD]).astype(jnp.bfloat16)
     out_ref[0, HEAD:end] = direct_ref[0, HEAD:end]
@@ -356,12 +333,12 @@
         in_specs=[
             pl.BlockSpec(values.shape, lambda f: (0, 0)),
             pl.BlockSpec((HEAD + TAIL, values.shape[0]), lambda f: (f, 0)),
-            pl.BlockSpec((1, 1, rows), lambda f: (f, 0, 0)),
+            pl.BlockSpec((focal_local, rows), lambda f: (0, 0)),
             block,
         ],
         out_specs=block,
         compiler_params=pltpu.CompilerParams(vmem_limit_bytes=12 << 20),
-    )(values, last, onset.reshape(focal_local, 1, rows), direct_focus)
+    )(values, last, onset, direct_focus)
 
 
 def shards(reflection, direct_focus, onset):
@@ -383,7 +360,7 @@
     def over(axis, value):
         return lax.all_to_all(value, axis, split_axis=0, concat_axis=0, tiled=True)
 
-    def apply_reflection(reflection, own, extra, orient, kind):
+    def apply_reflection(own, extra, orient, kind):
         other = lax.ppermute(own, "core", [(0, 1), (1, 0)])
         return product(reflection, own, other, core, extra, orient, kind, sets, halves, pairs)
 
@@ -392,23 +369,24 @@
         (jnp.asarray(to_edge), direct_focus, core, half, none, blank)
     )
     sent, mix, back = opening(
-        jnp.asarray(first), direct, jnp.asarray(mix), jnp.asarray(back), here, groups, pairs
-    )
+        jnp.asarray(first), direct, jnp.asarray(mix), jnp.asarray(back), here
+    )
+    sent = spread_out(sent, groups, pairs)
     tables = (to_edge, mix, back)
     sent = sent.reshape(groups * pairs, per * focal_local, rows)
     own = over(("x", "h", "pair"), sent)
-    values, start, reflection = apply_reflection(reflection, own, onset, 1.0, "first")
+    values, start = apply_reflection(own, onset, 1.0, "first")
     moving, all_onset = mixing(over(("x", "h"), values), tables, half, blank, True, halves, pairs)
     for step in range(1, 2 * ITERS):
         own = over(("h", "pair"), moving)
         if step == 2 * ITERS - 1:
-            (values,) = apply_reflection(reflection, own, none, -1.0, "last")
+            (values,) = apply_reflection(own, none, -1.0, "last")
             values = over(("x", "h"), values)
             break
         if step % 2:
-            (values,) = apply_reflection(reflection, own, none, -1.0, "plain")
+            (values,) = apply_reflection(own, none, -1.0, "plain")
         else:
-            (values,) = apply_reflection(reflection, own, start, 1.0, "update")
+            (values,) = apply_reflection(own, start, 1.0, "update")
         (moving,) = mixing(over(("x", "h"), values), tables, half, all_onset, False, halves, pairs)
     return finish(
         values.reshape(groups * per * focal_local, rows), jnp.asarray(last), onset, direct_focus

time: 239 us -> 233 us (0.975)
  blocking collectives: 180 us -> 191 us
  waiting for transfers between devices: 7.89 us -> 0.02 us
  Pallas kernels: 47 us -> 40.5 us
  starting transfers between devices: 3.38 us -> 0.02 us
    all_to_all x11 -> x12, blocking collectives: 180 us -> 191 us  [over(): return lax.all_to_all(value, axis, split_axis=0, concat_axis=0, tiled=True)]
    all_to_all x1 -> x0, waiting for transfers between devices: 7.88 us -> none  [over(): return lax.all_to_all(value, axis, split_axis=0, concat_axis=0, tiled=True)]
    pallas_call x6 -> x7, Pallas kernels: 20.3 us -> 15.5 us  [the longest x6 15.5 us: product(): pl.pallas_call(functools.partial(own_kernel, pairs, halves, first), out_s...]
    all_to_all x1 -> x0, starting transfers between devices: 3.36 us -> none  [over(): return lax.all_to_all(value, axis, split_axis=0, concat_axis=0, tiled=True)]
  transfers between devices with their start and end apart: 7 -> 6, of which waited for: 1 -> 0; matrix products, arithmetic and copies ran while one was open for 0% -> 0% of each run, Pallas kernels for 9% -> 7%
where the time goes in v3:
time: 233 us; the launch traced here: 232 us
  blocking collectives  191 us (82%)
  Pallas kernels  40.5 us (17%)
    all_to_all x12, blocking collectives, over(): return lax.all_to_all(value, axis, split_axis=0, concat_axis=0, tiled=True)  191 us
    pallas_call x6, Pallas kernels, product(): pl.pallas_call(functools.partial(other_kernel, pairs, halves, sets, orien...  16.1 us
    pallas_call x6, Pallas kernels, product(): pl.pallas_call(functools.partial(own_kernel, pairs, halves, first), out_s...  15.5 us
  transfers between devices with their start and end apart: 6, of which 0 were waited for; matrix products, arithmetic and copies ran while one was open for 0% of the time, Pallas kernels for 7%

profile of v3, /device:TPU:0, one launch (start us, length us, event | category | flops | bytes accessed | tf_op | source)
XLA Modules:
  0.0 232.1 jit_solution(11536125623908466779)
XLA Ops:
  0.0 2.7 %shard_map.82 = (bf16[128,384]{1,0:T(8,128)(2,1)S(1)}, bf16[256,512]{1,0:T(8,128)(2,1)S(1)}, bf16[128,544]{1,0:T(8,128)(2,1)S(1)}) custom-call(s32[1]{0:T(128)} %bitcast.2.set_ref, bf16[128,4096]{1,0:T(8,128)(2,1)} %constant.29.clone.first_ref, bf16[4,1024,384]{2,1,0:T(8,128)(2,1)} %direct_ref.2, bf16[4,256,512]{2,1,0:T(8,128)(2,1)} %constant.30.clone.mix_ref, ...), custom_call_target="tpu_custom_call" | custom-call | flops 402653184 | bytes 3145728 | tf_op jit(solution)/shard_map/pallas_call | solution.py:119
  2.8 0.1 shard_map.83
  2.9 27.6 %all_to_all.60.x_ref = bf16[64,16,384]{2,1,0:T(8,128)(2,1)S(1)} all-to-all(bf16[64,16,384]{2,1,0:T(8,128)(2,1)S(1)} %bitcast.7), channel_id=1, replica_groups=mesh['x'=4,'h'=2,'pair'=8,'core'=2] {'x','h','pair'}, dimensions={0} | all-to-all | bytes 1572864 | tf_op jit(solution)/shard_map/all_to_all | solution.py:361
  30.5 2.6 %shard_map.84.refs_3_ = f32[2,768,64]{2,1,0:T(8,128)S(1)} custom-call(s32[1]{0:T(128)} %bitcast.core_ref.refs_0_, bf16[2,2,384,6144]{3,2,1,0:T(8,128)(2,1)S(1)} %bitcast.6, bf16[64,16,384]{2,1,0:T(8,128)(2,1)S(1)} %all_to_all.60.x_ref), custom_call_target="tpu_custom_call" | custom-call | flops 603979776 | bytes 9437184 | tf_op jit(solution)/shard_map/pallas_call | solution.py:232
  33.2 2.7 %shard_map.85 = (bf16[8,72,384]{2,1,0:T(8,128)(2,1)S(1)}, f32[2,2,32,384]{3,2,1,0:T(8,128)S(1)}) custom-call(s32[1]{0:T(128)} %bitcast.core_ref.refs_0_, bf16[2,2,384,6144]{3,2,1,0:T(8,128)(2,1)S(1)} %bitcast.6, bf16[64,16,384]{2,1,0:T(8,128)(2,1)S(1)} %collective-permute-done.refs_2_, f32[2,768,64]{2,1,0:T(8,128)S(1)} %shard_map.84.refs_3_, ...), custom_call_target="tpu_custom_call" | custom-call | flops 603979776 | bytes 9437184 | tf_op jit(solution)/shard_map/pallas_call | solution.py:249
  35.8 14.0 %all_to_all.61.v_ref = bf16[8,72,384]{2,1,0:T(8,128)(2,1)S(1)} all-to-all(bf16[8,72,384]{2,1,0:T(8,128)(2,1)S(1)} %get-tuple-element.22), channel_id=1, replica_groups=mesh['x'=4,'h'=2,'pair'=8,'core'=2] {'x','h'}, dimensions={0} | all-to-all | bytes 884736 | tf_op jit(solution)/shard_map/all_to_all | solution.py:361
  49.8 0.7 shard_map.86
  50.6 16.6 %all_to_all.62.x_ref = bf16[16,64,384]{2,1,0:T(8,128)(2,1)S(1)} all-to-all(bf16[16,64,384]{2,1,0:T(8,128)(2,1)S(1)} %get-tuple-element.27), channel_id=1, replica_groups=mesh['x'=4,'h'=2,'pair'=8,'core'=2] {'h','pair'}, dimensions={0} | all-to-all | bytes 1572864 | tf_op jit(solution)/shard_map/all_to_all | solution.py:361
  67.1 2.6 %shard_map.87.refs_3_ = f32[2,768,64]{2,1,0:T(8,128)S(1)} custom-call(s32[1]{0:T(128)} %bitcast.core_ref.refs_0_, bf16[2,2,384,6144]{3,2,1,0:T(8,128)(2,1)S(1)} %bitcast.6, bf16[16,64,384]{2,1,0:T(8,128)(2,1)S(1)} %all_to_all.62.x_ref), custom_call_target="tpu_custom_call" | custom-call | flops 603979776 | bytes 9437184 | tf_op jit(solution)/shard_map/pallas_call | solution.py:232
  69.8 2.7 %shard_map.88 = bf16[8,64,384]{2,1,0:T(8,128)(2,1)S(1)} custom-call(s32[1]{0:T(128)} %bitcast.core_ref.refs_0_, bf16[2,2,384,6144]{3,2,1,0:T(8,128)(2,1)S(1)} %bitcast.6, bf16[16,64,384]{2,1,0:T(8,128)(2,1)S(1)} %collective-permute-done.1.refs_2_, f32[2,768,64]{2,1,0:T(8,128)S(1)} %shard_map.87.refs_3_, f32[8,128]{1,0:T(8,128)S(1)} %broadcast_in_dim.6.refs_4_), custom_call_target="tpu_custom_call" | custom-call | flops 603979776 | bytes 9437184 | tf_op jit(solution)/shard_map/pallas_call | solution.py:249
  72.4 13.8 %all_to_all.63.v_ref = bf16[8,64,384]{2,1,0:T(8,128)(2,1)S(1)} all-to-all(bf16[8,64,384]{2,1,0:T(8,128)(2,1)S(1)} %shard_map.88), channel_id=1, replica_groups=mesh['x'=4,'h'=2,'pair'=8,'core'=2] {'x','h'}, dimensions={0} | all-to-all | bytes 786432 | tf_op jit(solution)/shard_map/all_to_all | solution.py:361
  86.3 0.7 shard_map.89
  87.0 16.7 %all_to_all.64.x_ref = bf16[16,64,384]{2,1,0:T(8,128)(2,1)S(1)} all-to-all(bf16[16,64,384]{2,1,0:T(8,128)(2,1)S(1)} %shard_map.89), channel_id=1, replica_groups=mesh['x'=4,'h'=2,'pair'=8,'core'=2] {'h','pair'}, dimensions={0} | all-to-all | bytes 1572864 | tf_op jit(solution)/shard_map/all_to_all | solution.py:361
  103.7 2.6 %shard_map.90.refs_3_ = f32[2,768,64]{2,1,0:T(8,128)S(1)} custom-call(s32[1]{0:T(128)} %bitcast.core_ref.refs_0_, bf16[2,2,384,6144]{3,2,1,0:T(8,128)(2,1)S(1)} %bitcast.6, bf16[16,64,384]{2,1,0:T(8,128)(2,1)S(1)} %all_to_all.64.x_ref), custom_call_target="tpu_custom_call" | custom-call | flops 603979776 | bytes 9437184 | tf_op jit(solution)/shard_map/pallas_call | solution.py:232
  106.3 2.7 %shard_map.91 = bf16[8,64,384]{2,1,0:T(8,128)(2,1)S(1)} custom-call(s32[1]{0:T(128)} %bitcast.core_ref.refs_0_, bf16[2,2,384,6144]{3,2,1,0:T(8,128)(2,1)S(1)} %bitcast.6, bf16[16,64,384]{2,1,0:T(8,128)(2,1)S(1)} %collective-permute-done.2.refs_2_, f32[2,768,64]{2,1,0:T(8,128)S(1)} %shard_map.90.refs_3_, f32[2,2,32,384]{3,2,1,0:T(8,128)S(1)} %get-tuple-element.30.refs_4_), custom_call_target="tpu_custom_call" | custom-call | flops 603979776 | bytes 9437184 | tf_op jit(solution)/shard_map/pallas_call | solution.py:249
  109.0 13.8 %all_to_all.65.v_ref = bf16[8,64,384]{2,1,0:T(8,128)(2,1)S(1)} all-to-all(bf16[8,64,384]{2,1,0:T(8,128)(2,1)S(1)} %shard_map.91), channel_id=1, replica_groups=mesh['x'=4,'h'=2,'pair'=8,'core'=2] {'x','h'}, dimensions={0} | all-to-all | bytes 786432 | tf_op jit(solution)/shard_map/all_to_all | solution.py:361
  122.8 0.7 shard_map.92
  123.6 16.7 %all_to_all.66.x_ref = bf16[16,64,384]{2,1,0:T(8,128)(2,1)S(1)} all-to-all(bf16[16,64,384]{2,1,0:T(8,128)(2,1)S(1)} %shard_map.92), channel_id=1, replica_groups=mesh['x'=4,'h'=2,'pair'=8,'core'=2] {'h','pair'}, dimensions={0} | all-to-all | bytes 1572864 | tf_op jit(solution)/shard_map/all_to_all | solution.py:361
  140.3 2.6 %shard_map.93.refs_3_ = f32[2,768,64]{2,1,0:T(8,128)S(1)} custom-call(s32[1]{0:T(128)} %bitcast.core_ref.refs_0_, bf16[2,2,384,6144]{3,2,1,0:T(8,128)(2,1)S(1)} %bitcast.6, bf16[16,64,384]{2,1,0:T(8,128)(2,1)S(1)} %all_to_all.66.x_ref), custom_call_target="tpu_custom_call" | custom-call | flops 603979776 | bytes 9437184 | tf_op jit(solution)/shard_map/pallas_call | solution.py:232
  142.9 2.7 %shard_map.94 = bf16[8,64,384]{2,1,0:T(8,128)(2,1)S(1)} custom-call(s32[1]{0:T(128)} %bitcast.core_ref.refs_0_, bf16[2,2,384,6144]{3,2,1,0:T(8,128)(2,1)S(1)} %bitcast.6, bf16[16,64,384]{2,1,0:T(8,128)(2,1)S(1)} %collective-permute-done.3.refs_2_, f32[2,768,64]{2,1,0:T(8,128)S(1)} %shard_map.93.refs_3_, f32[8,128]{1,0:T(8,128)S(1)} %broadcast_in_dim.6.refs_4_), custom_call_target="tpu_custom_call" | custom-call | flops 603979776 | bytes 9437184 | tf_op jit(solution)/shard_map/pallas_call | solution.py:249
  145.6 13.8 %all_to_all.67.v_ref = bf16[8,64,384]{2,1,0:T(8,128)(2,1)S(1)} all-to-all(bf16[8,64,384]{2,1,0:T(8,128)(2,1)S(1)} %shard_map.94), channel_id=1, replica_groups=mesh['x'=4,'h'=2,'pair'=8,'core'=2] {'x','h'}, dimensions={0} | all-to-all | bytes 786432 | tf_op jit(solution)/shard_map/all_to_all | solution.py:361
  159.4 0.7 shard_map.95
  160.1 16.7 %all_to_all.68.x_ref = bf16[16,64,384]{2,1,0:T(8,128)(2,1)S(1)} all-to-all(bf16[16,64,384]{2,1,0:T(8,128)(2,1)S(1)} %shard_map.95), channel_id=1, replica_groups=mesh['x'=4,'h'=2,'pair'=8,'core'=2] {'h','pair'}, dimensions={0} | all-to-all | bytes 1572864 | tf_op jit(solution)/shard_map/all_to_all | solution.py:361
  176.8 2.6 %shard_map.96.refs_3_ = f32[2,768,64]{2,1,0:T(8,128)S(1)} custom-call(s32[1]{0:T(128)} %bitcast.core_ref.refs_0_, bf16[2,2,384,6144]{3,2,1,0:T(8,128)(2,1)S(1)} %bitcast.6, bf16[16,64,384]{2,1,0:T(8,128)(2,1)S(1)} %all_to_all.68.x_ref), custom_call_target="tpu_custom_call" | custom-call | flops 603979776 | bytes 9437184 | tf_op jit(solution)/shard_map/pallas_call | solution.py:232
  179.4 2.7 %shard_map.97 = bf16[8,64,384]{2,1,0:T(8,128)(2,1)S(1)} custom-call(s32[1]{0:T(128)} %bitcast.core_ref.refs_0_, bf16[2,2,384,6144]{3,2,1,0:T(8,128)(2,1)S(1)} %bitcast.6, bf16[16,64,384]{2,1,0:T(8,128)(2,1)S(1)} %collective-permute-done.4.refs_2_, f32[2,768,64]{2,1,0:T(8,128)S(1)} %shard_map.96.refs_3_, f32[2,2,32,384]{3,2,1,0:T(8,128)S(1)} %get-tuple-element.30.refs_4_), custom_call_target="tpu_custom_call" | custom-call | flops 603979776 | bytes 9437184 | tf_op jit(solution)/shard_map/pallas_call | solution.py:249
  182.1 13.8 %all_to_all.69.v_ref = bf16[8,64,384]{2,1,0:T(8,128)(2,1)S(1)} all-to-all(bf16[8,64,384]{2,1,0:T(8,128)(2,1)S(1)} %shard_map.97), channel_id=1, replica_groups=mesh['x'=4,'h'=2,'pair'=8,'core'=2] {'x','h'}, dimensions={0} | all-to-all | bytes 786432 | tf_op jit(solution)/shard_map/all_to_all | solution.py:361
  196.0 0.7 shard_map.98
  196.7 16.7 %all_to_all.70.x_ref = bf16[16,64,384]{2,1,0:T(8,128)(2,1)S(1)} all-to-all(bf16[16,64,384]{2,1,0:T(8,128)(2,1)S(1)} %shard_map.98), channel_id=1, replica_groups=mesh['x'=4,'h'=2,'pair'=8,'core'=2] {'h','pair'}, dimensions={0} | all-to-all | bytes 1572864 | tf_op jit(solution)/shard_map/all_to_all | solution.py:361
  213.4 2.6 %shard_map.99.refs_3_ = f32[2,768,64]{2,1,0:T(8,128)S(1)} custom-call(s32[1]{0:T(128)} %bitcast.core_ref.refs_0_, bf16[2,2,384,6144]{3,2,1,0:T(8,128)(2,1)S(1)} %bitcast.6, bf16[16,64,384]{2,1,0:T(8,128)(2,1)S(1)} %all_to_all.70.x_ref), custom_call_target="tpu_custom_call" | custom-call | flops 603979776 | bytes 9437184 | tf_op jit(solution)/shard_map/pallas_call | solution.py:232
  216.0 2.7 %shard_map.100 = bf16[8,16,384]{2,1,0:T(8,128)(2,1)S(1)} custom-call(s32[1]{0:T(128)} %bitcast.core_ref.refs_0_, bf16[2,2,384,6144]{3,2,1,0:T(8,128)(2,1)S(1)} %bitcast.6, bf16[16,64,384]{2,1,0:T(8,128)(2,1)S(1)} %collective-permute-done.5.refs_2_, f32[2,768,64]{2,1,0:T(8,128)S(1)} %shard_map.99.refs_3_, f32[8,128]{1,0:T(8,128)S(1)} %broadcast_in_dim.6.refs_4_), custom_call_target="tpu_custom_call" | custom-call | flops 603979776 | bytes 9437184 | tf_op jit(solution)/shard_map/pallas_call | solution.py:249
  218.7 11.0 %all_to_all.71 = bf16[8,16,384]{2,1,0:T(8,128)(2,1)S(1)} all-to-all(bf16[8,16,384]{2,1,0:T(8,128)(2,1)S(1)} %shard_map.100), channel_id=1, replica_groups=mesh['x'=4,'h'=2,'pair'=8,'core'=2] {'x','h'}, dimensions={0} | all-to-all | bytes 196608 | tf_op jit(solution)/shard_map/all_to_all | solution.py:361
  229.7 2.4 %shard_map.101 = bf16[4,1024,384]{2,1,0:T(8,128)(2,1)} custom-call(bf16[128,384]{1,0:T(8,128)(2,1)S(1)} %bitcast.8, bf16[704,128]{1,0:T(8,128)(2,1)S(1)} %copy-done.2, s32[4,384]{1,0:T(4,128)S(1)} %copy-done.3, bf16[4,1024,384]{2,1,0:T(8,128)(2,1)S(1)} %copy-done.1), custom_call_target="tpu_custom_call" | custom-call | tf_op jit(solution)/shard_map/pallas_call | solution.py:329
  (33 shorter events, 0.1 us)
Async XLA Ops:
  2.7 27.7 %slice-start = ((s8[18874368]{0:T(1024)(128)(4,1)}), s8[4194304]{0:T(1024)(128)(4,1)S(1)}, s32[]{:S(2)}) async-start(s8[18874368]{0:T(1024)(128)(4,1)} %bitcast.5), calls=%async_computation.12 | async-start | bytes 8388608
  2.8 27.7 %slice-start.1 = ((s8[18874368]{0:T(1024)(128)(4,1)}), s8[4194304]{0:T(1024)(128)(4,1)S(1)}, s32[]{:S(2)}) async-start(s8[18874368]{0:T(1024)(128)(4,1)} %bitcast.5), calls=%async_computation.13 | async-start | bytes 8388608
  2.8 27.7 %slice-start.2 = ((s8[18874368]{0:T(1024)(128)(4,1)}), s8[4194304]{0:T(1024)(128)(4,1)S(1)}, s32[]{:S(2)}) async-start(s8[18874368]{0:T(1024)(128)(4,1)} %bitcast.5), calls=%async_computation.14 | async-start | bytes 8388608
  2.8 27.7 %slice-start.3 = ((s8[18874368]{0:T(1024)(128)(4,1)}), s8[4194304]{0:T(1024)(128)(4,1)S(1)}, s32[]{:S(2)}) async-start(s8[18874368]{0:T(1024)(128)(4,1)} %bitcast.5), calls=%async_computation.15 | async-start | bytes 8388608
  2.8 27.7 %slice-start.4 = ((s8[18874368]{0:T(1024)(128)(4,1)}), s8[2097152]{0:T(1024)(128)(4,1)S(1)}, s32[]{:S(2)}) async-start(s8[18874368]{0:T(1024)(128)(4,1)} %bitcast.5), calls=%async_computation.16 | async-start | bytes 4194304
  30.5 2.7 %copy-start.3 = (s32[4,384]{1,0:T(4,128)S(1)}, s32[4,384]{1,0:T(4,128)}, u32[]{:S(2)}) copy-start(s32[4,384]{1,0:T(4,128)} %onset_ref.1) | copy-start | bytes 18436
  30.5 2.7 %collective-permute-start = (bf16[64,16,384]{2,1,0:T(8,128)(2,1)S(1)}, bf16[64,16,384]{2,1,0:T(8,128)(2,1)S(1)}, u32[]{:S(2)}, u32[]{:S(2)}) collective-permute-start(bf16[64,16,384]{2,1,0:T(8,128)(2,1)S(1)} %all_to_all.60.x_ref), channel_id=1, source_target_pairs={{0,1},{1,0},{2,3},{3,2},{4,5},{5,4},{6,7},{7,6},{8,9},{9,8},{10,11... | collective-permute-start | bytes 2359304 | tf_op jit(solution)/shard_map/ppermute | solution.py:364
  33.1 16.7 %copy-start = (bf16[544,512]{1,0:T(8,128)(2,1)S(1)}, bf16[544,512]{1,0:T(8,128)(2,1)}, u32[]{:S(2)}) copy-start(bf16[544,512]{1,0:T(8,128)(2,1)} %constant.28.clone.edge_ref) | copy-start | bytes 1671172
  67.1 2.6 %collective-permute-start.1 = (bf16[16,64,384]{2,1,0:T(8,128)(2,1)S(1)}, bf16[16,64,384]{2,1,0:T(8,128)(2,1)S(1)}, u32[]{:S(2)}, u32[]{:S(2)}) collective-permute-start(bf16[16,64,384]{2,1,0:T(8,128)(2,1)S(1)} %all_to_all.62.x_ref), channel_id=1, source_target_pairs={{0,1},{1,0},{2,3},{3,2},{4,5},{5,4},{6,7},{7,6},{8,9},{9,8},{10,11... | collective-permute-start | bytes 2359304 | tf_op jit(solution)/shard_map/ppermute | solution.py:364
  103.7 2.6 %collective-permute-start.2 = (bf16[16,64,384]{2,1,0:T(8,128)(2,1)S(1)}, bf16[16,64,384]{2,1,0:T(8,128)(2,1)S(1)}, u32[]{:S(2)}, u32[]{:S(2)}) collective-permute-start(bf16[16,64,384]{2,1,0:T(8,128)(2,1)S(1)} %all_to_all.64.x_ref), channel_id=1, source_target_pairs={{0,1},{1,0},{2,3},{3,2},{4,5},{5,4},{6,7},{7,6},{8,9},{9,8},{10,11... | collective-permute-start | bytes 2359304 | tf_op jit(solution)/shard_map/ppermute | solution.py:364
  140.3 2.6 %collective-permute-start.3 = (bf16[16,64,384]{2,1,0:T(8,128)(2,1)S(1)}, bf16[16,64,384]{2,1,0:T(8,128)(2,1)S(1)}, u32[]{:S(2)}, u32[]{:S(2)}) collective-permute-start(bf16[16,64,384]{2,1,0:T(8,128)(2,1)S(1)} %all_to_all.66.x_ref), channel_id=1, source_target_pairs={{0,1},{1,0},{2,3},{3,2},{4,5},{5,4},{6,7},{7,6},{8,9},{9,8},{10,11... | collective-permute-start | bytes 2359304 | tf_op jit(solution)/shard_map/ppermute | solution.py:364
  176.8 2.6 %collective-permute-start.4 = (bf16[16,64,384]{2,1,0:T(8,128)(2,1)S(1)}, bf16[16,64,384]{2,1,0:T(8,128)(2,1)S(1)}, u32[]{:S(2)}, u32[]{:S(2)}) collective-permute-start(bf16[16,64,384]{2,1,0:T(8,128)(2,1)S(1)} %all_to_all.68.x_ref), channel_id=1, source_target_pairs={{0,1},{1,0},{2,3},{3,2},{4,5},{5,4},{6,7},{7,6},{8,9},{9,8},{10,11... | collective-permute-start | bytes 2359304 | tf_op jit(solution)/shard_map/ppermute | solution.py:364
  213.4 2.6 %collective-permute-start.5 = (bf16[16,64,384]{2,1,0:T(8,128)(2,1)S(1)}, bf16[16,64,384]{2,1,0:T(8,128)(2,1)S(1)}, u32[]{:S(2)}, u32[]{:S(2)}) collective-permute-start(bf16[16,64,384]{2,1,0:T(8,128)(2,1)S(1)} %all_to_all.70.x_ref), channel_id=1, source_target_pairs={{0,1},{1,0},{2,3},{3,2},{4,5},{5,4},{6,7},{7,6},{8,9},{9,8},{10,11... | collective-permute-start | bytes 2359304 | tf_op jit(solution)/shard_map/ppermute | solution.py:364
  216.0 13.7 %copy-start.1 = (bf16[4,1024,384]{2,1,0:T(8,128)(2,1)S(1)}, bf16[4,1024,384]{2,1,0:T(8,128)(2,1)}, u32[]{:S(2)}) copy-start(bf16[4,1024,384]{2,1,0:T(8,128)(2,1)} %direct_ref.2) | copy-start | bytes 9437188
  216.0 13.7 %copy-start.2 = (bf16[704,128]{1,0:T(8,128)(2,1)S(1)}, bf16[704,128]{1,0:T(8,128)(2,1)}, u32[]{:S(2)}) copy-start(bf16[704,128]{1,0:T(8,128)(2,1)} %constant.32.clone.last_ref) | copy-start | bytes 540676

commit v4 on v3

--- a/solution.py
+++ b/solution.py
@@ -311,33 +311,52 @@
     )(half, values, *tables, onset)
 
 
-def finish_kernel(values_ref, last_ref, onset_ref, direct_ref, out_ref):
-    _, count_time, rows = direct_ref.shape
-    change = jnp.dot(last_ref[...], values_ref[...], preferred_element_type=jnp.float32)
-    number = lax.broadcasted_iota(jnp.int32, change.shape, 0)
-    distance = jnp.where(number < HEAD, number, HEAD + TAIL - number)
-    change = jnp.where(distance < onset_ref[pl.ds(pl.program_id(0), 1), :], change, 0.0)
+def finish_kernel(values_ref, last_ref, onset_ref, direct_ref, out_ref, ends_ref, sems):
+    focal_local, count_time, _ = direct_ref.shape
     end = count_time - TAIL
-    out_ref[0, :HEAD] = (direct_ref[0, :HEAD].astype(jnp.float32) - change[:HEAD]).astype(jnp.bfloat16)
-    out_ref[0, HEAD:end] = direct_ref[0, HEAD:end]
-    out_ref[0, end:] = (direct_ref[0, end:].astype(jnp.float32) - change[HEAD:]).astype(jnp.bfloat16)
+    count = HEAD + TAIL
+    copies = [
+        pltpu.make_async_copy(
+            direct_ref.at[:, HEAD:end], out_ref.at[:, HEAD:end], sems.at[2 * focal_local]
+        )
+    ]
+    copies[0].start()
+    for f in range(focal_local):
+        change = jnp.dot(
+            last_ref[f * count : (f + 1) * count], values_ref[...], preferred_element_type=jnp.float32
+        )
+        number = lax.broadcasted_iota(jnp.int32, change.shape, 0)
+        distance = jnp.where(number < HEAD, number, count - number)
+        change = jnp.where(distance < onset_ref[f : f + 1, :], change, 0.0)
+        head = direct_ref[f, :HEAD].astype(jnp.float32) - change[:HEAD]
+        tail = direct_ref[f, end:].astype(jnp.float32) - change[HEAD:]
+        ends_ref[f, :HEAD] = head.astype(jnp.bfloat16)
+        ends_ref[f, HEAD:] = tail.astype(jnp.bfloat16)
+        for n, (rows, place) in enumerate(
+            ((slice(0, HEAD), slice(0, HEAD)), (slice(HEAD, count), slice(end, count_time)))
+        ):
+            copy = pltpu.make_async_copy(
+                ends_ref.at[f, rows], out_ref.at[f, place], sems.at[2 * f + n]
+            )
+            copy.start()
+            copies.append(copy)
+    for copy in copies:
+        copy.wait()
 
 
 def finish(values, last, onset, direct_focus):
-    focal_local, count_time, rows = direct_focus.shape
-    block = pl.BlockSpec((1, count_time, rows), lambda f: (f, 0, 0))
+    focal_local, _, rows = direct_focus.shape
+    local = pl.BlockSpec(memory_space=pltpu.VMEM)
     return pl.pallas_call(
         finish_kernel,
         out_shape=jax.ShapeDtypeStruct(direct_focus.shape, jnp.bfloat16),
-        grid=(focal_local,),
-        in_specs=[
-            pl.BlockSpec(values.shape, lambda f: (0, 0)),
-            pl.BlockSpec((HEAD + TAIL, values.shape[0]), lambda f: (f, 0)),
-            pl.BlockSpec((focal_local, rows), lambda f: (0, 0)),
-            block,
+        in_specs=[local] * 4,
+        out_specs=pl.BlockSpec(memory_space=pltpu.HBM),
+        scratch_shapes=[
+            pltpu.VMEM((focal_local, HEAD + TAIL, rows), jnp.bfloat16),
+            pltpu.SemaphoreType.DMA((2 * focal_local + 1,)),
         ],
-        out_specs=block,
-        compiler_params=pltpu.CompilerParams(vmem_limit_bytes=12 << 20),
+        compiler_params=pltpu.CompilerParams(vmem_limit_bytes=8 << 20),
     )(values, last, onset, direct_focus)
 
 

time: 233 us -> 232 us (level)
  no operation moved by 1% of the time
where the time goes in v4:
time: 232 us
  blocking collectives  191 us (82%)
  Pallas kernels  39.8 us (17%)
    all_to_all x12, blocking collectives, over(): return lax.all_to_all(value, axis, split_axis=0, concat_axis=0, tiled=True)  191 us
    pallas_call x6, Pallas kernels, product(): pl.pallas_call(functools.partial(other_kernel, pairs, halves, sets, orien...  16.1 us
    pallas_call x6, Pallas kernels, product(): pl.pallas_call(functools.partial(own_kernel, pairs, halves, first), out_s...  15.5 us
  transfers between devices with their start and end apart: 6, of which 0 were waited for; matrix products, arithmetic and copies ran while one was open for 0% of the time, Pallas kernels for 7%

profile of v4, /device:TPU:0, one launch (start us, length us, event | category | flops | bytes accessed | tf_op | source)
XLA Modules:
  0.0 231.6 jit_solution(2377348088278671726)
XLA Ops:
  0.0 2.7 %shard_map.82 = (bf16[128,384]{1,0:T(8,128)(2,1)S(1)}, bf16[256,512]{1,0:T(8,128)(2,1)S(1)}, bf16[128,544]{1,0:T(8,128)(2,1)S(1)}) custom-call(s32[1]{0:T(128)} %bitcast.2.set_ref, bf16[128,4096]{1,0:T(8,128)(2,1)} %constant.29.clone.first_ref, bf16[4,1024,384]{2,1,0:T(8,128)(2,1)} %direct_ref.2, bf16[4,256,512]{2,1,0:T(8,128)(2,1)} %constant.30.clone.mix_ref, ...), custom_call_target="tpu_custom_call" | custom-call | flops 402653184 | bytes 3145728 | tf_op jit(solution)/shard_map/pallas_call | solution.py:119
  2.8 0.1 shard_map.83
  2.9 27.6 %all_to_all.60.x_ref = bf16[64,16,384]{2,1,0:T(8,128)(2,1)S(1)} all-to-all(bf16[64,16,384]{2,1,0:T(8,128)(2,1)S(1)} %bitcast.7), channel_id=1, replica_groups=mesh['x'=4,'h'=2,'pair'=8,'core'=2] {'x','h','pair'}, dimensions={0} | all-to-all | bytes 1572864 | tf_op jit(solution)/shard_map/all_to_all | solution.py:380
  30.5 2.6 %shard_map.84.refs_3_ = f32[2,768,64]{2,1,0:T(8,128)S(1)} custom-call(s32[1]{0:T(128)} %bitcast.core_ref.refs_0_, bf16[2,2,384,6144]{3,2,1,0:T(8,128)(2,1)S(1)} %bitcast.6, bf16[64,16,384]{2,1,0:T(8,128)(2,1)S(1)} %all_to_all.60.x_ref), custom_call_target="tpu_custom_call" | custom-call | flops 603979776 | bytes 9437184 | tf_op jit(solution)/shard_map/pallas_call | solution.py:232
  33.2 2.7 %shard_map.85 = (bf16[8,72,384]{2,1,0:T(8,128)(2,1)S(1)}, f32[2,2,32,384]{3,2,1,0:T(8,128)S(1)}) custom-call(s32[1]{0:T(128)} %bitcast.core_ref.refs_0_, bf16[2,2,384,6144]{3,2,1,0:T(8,128)(2,1)S(1)} %bitcast.6, bf16[64,16,384]{2,1,0:T(8,128)(2,1)S(1)} %collective-permute-done.refs_2_, f32[2,768,64]{2,1,0:T(8,128)S(1)} %shard_map.84.refs_3_, ...), custom_call_target="tpu_custom_call" | custom-call | flops 603979776 | bytes 9437184 | tf_op jit(solution)/shard_map/pallas_call | solution.py:249
  35.8 14.0 %all_to_all.61.v_ref = bf16[8,72,384]{2,1,0:T(8,128)(2,1)S(1)} all-to-all(bf16[8,72,384]{2,1,0:T(8,128)(2,1)S(1)} %get-tuple-element.22), channel_id=1, replica_groups=mesh['x'=4,'h'=2,'pair'=8,'core'=2] {'x','h'}, dimensions={0} | all-to-all | bytes 884736 | tf_op jit(solution)/shard_map/all_to_all | solution.py:380
  49.8 0.7 shard_map.86
  50.6 16.6 %all_to_all.62.x_ref = bf16[16,64,384]{2,1,0:T(8,128)(2,1)S(1)} all-to-all(bf16[16,64,384]{2,1,0:T(8,128)(2,1)S(1)} %get-tuple-element.27), channel_id=1, replica_groups=mesh['x'=4,'h'=2,'pair'=8,'core'=2] {'h','pair'}, dimensions={0} | all-to-all | bytes 1572864 | tf_op jit(solution)/shard_map/all_to_all | solution.py:380
  67.1 2.6 %shard_map.87.refs_3_ = f32[2,768,64]{2,1,0:T(8,128)S(1)} custom-call(s32[1]{0:T(128)} %bitcast.core_ref.refs_0_, bf16[2,2,384,6144]{3,2,1,0:T(8,128)(2,1)S(1)} %bitcast.6, bf16[16,64,384]{2,1,0:T(8,128)(2,1)S(1)} %all_to_all.62.x_ref), custom_call_target="tpu_custom_call" | custom-call | flops 603979776 | bytes 9437184 | tf_op jit(solution)/shard_map/pallas_call | solution.py:232
  69.8 2.7 %shard_map.88 = bf16[8,64,384]{2,1,0:T(8,128)(2,1)S(1)} custom-call(s32[1]{0:T(128)} %bitcast.core_ref.refs_0_, bf16[2,2,384,6144]{3,2,1,0:T(8,128)(2,1)S(1)} %bitcast.6, bf16[16,64,384]{2,1,0:T(8,128)(2,1)S(1)} %collective-permute-done.1.refs_2_, f32[2,768,64]{2,1,0:T(8,128)S(1)} %shard_map.87.refs_3_, f32[8,128]{1,0:T(8,128)S(1)} %broadcast_in_dim.6.refs_4_), custom_call_target="tpu_custom_call" | custom-call | flops 603979776 | bytes 9437184 | tf_op jit(solution)/shard_map/pallas_call | solution.py:249
  72.4 13.8 %all_to_all.63.v_ref = bf16[8,64,384]{2,1,0:T(8,128)(2,1)S(1)} all-to-all(bf16[8,64,384]{2,1,0:T(8,128)(2,1)S(1)} %shard_map.88), channel_id=1, replica_groups=mesh['x'=4,'h'=2,'pair'=8,'core'=2] {'x','h'}, dimensions={0} | all-to-all | bytes 786432 | tf_op jit(solution)/shard_map/all_to_all | solution.py:380
  86.3 0.7 shard_map.89
  87.0 16.7 %all_to_all.64.x_ref = bf16[16,64,384]{2,1,0:T(8,128)(2,1)S(1)} all-to-all(bf16[16,64,384]{2,1,0:T(8,128)(2,1)S(1)} %shard_map.89), channel_id=1, replica_groups=mesh['x'=4,'h'=2,'pair'=8,'core'=2] {'h','pair'}, dimensions={0} | all-to-all | bytes 1572864 | tf_op jit(solution)/shard_map/all_to_all | solution.py:380
  103.7 2.6 %shard_map.90.refs_3_ = f32[2,768,64]{2,1,0:T(8,128)S(1)} custom-call(s32[1]{0:T(128)} %bitcast.core_ref.refs_0_, bf16[2,2,384,6144]{3,2,1,0:T(8,128)(2,1)S(1)} %bitcast.6, bf16[16,64,384]{2,1,0:T(8,128)(2,1)S(1)} %all_to_all.64.x_ref), custom_call_target="tpu_custom_call" | custom-call | flops 603979776 | bytes 9437184 | tf_op jit(solution)/shard_map/pallas_call | solution.py:232
  106.3 2.7 %shard_map.91 = bf16[8,64,384]{2,1,0:T(8,128)(2,1)S(1)} custom-call(s32[1]{0:T(128)} %bitcast.core_ref.refs_0_, bf16[2,2,384,6144]{3,2,1,0:T(8,128)(2,1)S(1)} %bitcast.6, bf16[16,64,384]{2,1,0:T(8,128)(2,1)S(1)} %collective-permute-done.2.refs_2_, f32[2,768,64]{2,1,0:T(8,128)S(1)} %shard_map.90.refs_3_, f32[2,2,32,384]{3,2,1,0:T(8,128)S(1)} %get-tuple-element.30.refs_4_), custom_call_target="tpu_custom_call" | custom-call | flops 603979776 | bytes 9437184 | tf_op jit(solution)/shard_map/pallas_call | solution.py:249
  109.0 13.8 %all_to_all.65.v_ref = bf16[8,64,384]{2,1,0:T(8,128)(2,1)S(1)} all-to-all(bf16[8,64,384]{2,1,0:T(8,128)(2,1)S(1)} %shard_map.91), channel_id=1, replica_groups=mesh['x'=4,'h'=2,'pair'=8,'core'=2] {'x','h'}, dimensions={0} | all-to-all | bytes 786432 | tf_op jit(solution)/shard_map/all_to_all | solution.py:380
  122.8 0.7 shard_map.92
  123.5 16.7 %all_to_all.66.x_ref = bf16[16,64,384]{2,1,0:T(8,128)(2,1)S(1)} all-to-all(bf16[16,64,384]{2,1,0:T(8,128)(2,1)S(1)} %shard_map.92), channel_id=1, replica_groups=mesh['x'=4,'h'=2,'pair'=8,'core'=2] {'h','pair'}, dimensions={0} | all-to-all | bytes 1572864 | tf_op jit(solution)/shard_map/all_to_all | solution.py:380
  140.3 2.6 %shard_map.93.refs_3_ = f32[2,768,64]{2,1,0:T(8,128)S(1)} custom-call(s32[1]{0:T(128)} %bitcast.core_ref.refs_0_, bf16[2,2,384,6144]{3,2,1,0:T(8,128)(2,1)S(1)} %bitcast.6, bf16[16,64,384]{2,1,0:T(8,128)(2,1)S(1)} %all_to_all.66.x_ref), custom_call_target="tpu_custom_call" | custom-call | flops 603979776 | bytes 9437184 | tf_op jit(solution)/shard_map/pallas_call | solution.py:232
  142.9 2.7 %shard_map.94 = bf16[8,64,384]{2,1,0:T(8,128)(2,1)S(1)} custom-call(s32[1]{0:T(128)} %bitcast.core_ref.refs_0_, bf16[2,2,384,6144]{3,2,1,0:T(8,128)(2,1)S(1)} %bitcast.6, bf16[16,64,384]{2,1,0:T(8,128)(2,1)S(1)} %collective-permute-done.3.refs_2_, f32[2,768,64]{2,1,0:T(8,128)S(1)} %shard_map.93.refs_3_, f32[8,128]{1,0:T(8,128)S(1)} %broadcast_in_dim.6.refs_4_), custom_call_target="tpu_custom_call" | custom-call | flops 603979776 | bytes 9437184 | tf_op jit(solution)/shard_map/pallas_call | solution.py:249
  145.5 13.8 %all_to_all.67.v_ref = bf16[8,64,384]{2,1,0:T(8,128)(2,1)S(1)} all-to-all(bf16[8,64,384]{2,1,0:T(8,128)(2,1)S(1)} %shard_map.94), channel_id=1, replica_groups=mesh['x'=4,'h'=2,'pair'=8,'core'=2] {'x','h'}, dimensions={0} | all-to-all | bytes 786432 | tf_op jit(solution)/shard_map/all_to_all | solution.py:380
  159.4 0.7 shard_map.95
  160.1 16.7 %all_to_all.68.x_ref = bf16[16,64,384]{2,1,0:T(8,128)(2,1)S(1)} all-to-all(bf16[16,64,384]{2,1,0:T(8,128)(2,1)S(1)} %shard_map.95), channel_id=1, replica_groups=mesh['x'=4,'h'=2,'pair'=8,'core'=2] {'h','pair'}, dimensions={0} | all-to-all | bytes 1572864 | tf_op jit(solution)/shard_map/all_to_all | solution.py:380
  176.8 2.6 %shard_map.96.refs_3_ = f32[2,768,64]{2,1,0:T(8,128)S(1)} custom-call(s32[1]{0:T(128)} %bitcast.core_ref.refs_0_, bf16[2,2,384,6144]{3,2,1,0:T(8,128)(2,1)S(1)} %bitcast.6, bf16[16,64,384]{2,1,0:T(8,128)(2,1)S(1)} %all_to_all.68.x_ref), custom_call_target="tpu_custom_call" | custom-call | flops 603979776 | bytes 9437184 | tf_op jit(solution)/shard_map/pallas_call | solution.py:232
  179.4 2.7 %shard_map.97 = bf16[8,64,384]{2,1,0:T(8,128)(2,1)S(1)} custom-call(s32[1]{0:T(128)} %bitcast.core_ref.refs_0_, bf16[2,2,384,6144]{3,2,1,0:T(8,128)(2,1)S(1)} %bitcast.6, bf16[16,64,384]{2,1,0:T(8,128)(2,1)S(1)} %collective-permute-done.4.refs_2_, f32[2,768,64]{2,1,0:T(8,128)S(1)} %shard_map.96.refs_3_, f32[2,2,32,384]{3,2,1,0:T(8,128)S(1)} %get-tuple-element.30.refs_4_), custom_call_target="tpu_custom_call" | custom-call | flops 603979776 | bytes 9437184 | tf_op jit(solution)/shard_map/pallas_call | solution.py:249
  182.1 13.8 %all_to_all.69.v_ref = bf16[8,64,384]{2,1,0:T(8,128)(2,1)S(1)} all-to-all(bf16[8,64,384]{2,1,0:T(8,128)(2,1)S(1)} %shard_map.97), channel_id=1, replica_groups=mesh['x'=4,'h'=2,'pair'=8,'core'=2] {'x','h'}, dimensions={0} | all-to-all | bytes 786432 | tf_op jit(solution)/shard_map/all_to_all | solution.py:380
  195.9 0.7 shard_map.98
  196.6 16.7 %all_to_all.70.x_ref = bf16[16,64,384]{2,1,0:T(8,128)(2,1)S(1)} all-to-all(bf16[16,64,384]{2,1,0:T(8,128)(2,1)S(1)} %shard_map.98), channel_id=1, replica_groups=mesh['x'=4,'h'=2,'pair'=8,'core'=2] {'h','pair'}, dimensions={0} | all-to-all | bytes 1572864 | tf_op jit(solution)/shard_map/all_to_all | solution.py:380
  213.4 2.6 %shard_map.99.refs_3_ = f32[2,768,64]{2,1,0:T(8,128)S(1)} custom-call(s32[1]{0:T(128)} %bitcast.core_ref.refs_0_, bf16[2,2,384,6144]{3,2,1,0:T(8,128)(2,1)S(1)} %bitcast.6, bf16[16,64,384]{2,1,0:T(8,128)(2,1)S(1)} %all_to_all.70.x_ref), custom_call_target="tpu_custom_call" | custom-call | flops 603979776 | bytes 9437184 | tf_op jit(solution)/shard_map/pallas_call | solution.py:232
  216.0 2.7 %shard_map.100 = bf16[8,16,384]{2,1,0:T(8,128)(2,1)S(1)} custom-call(s32[1]{0:T(128)} %bitcast.core_ref.refs_0_, bf16[2,2,384,6144]{3,2,1,0:T(8,128)(2,1)S(1)} %bitcast.6, bf16[16,64,384]{2,1,0:T(8,128)(2,1)S(1)} %collective-permute-done.5.refs_2_, f32[2,768,64]{2,1,0:T(8,128)S(1)} %shard_map.99.refs_3_, f32[8,128]{1,0:T(8,128)S(1)} %broadcast_in_dim.6.refs_4_), custom_call_target="tpu_custom_call" | custom-call | flops 603979776 | bytes 9437184 | tf_op jit(solution)/shard_map/pallas_call | solution.py:249
  218.7 11.0 %all_to_all.71 = bf16[8,16,384]{2,1,0:T(8,128)(2,1)S(1)} all-to-all(bf16[8,16,384]{2,1,0:T(8,128)(2,1)S(1)} %shard_map.100), channel_id=1, replica_groups=mesh['x'=4,'h'=2,'pair'=8,'core'=2] {'x','h'}, dimensions={0} | all-to-all | bytes 196608 | tf_op jit(solution)/shard_map/all_to_all | solution.py:380
  229.7 1.7 shard_map.101
  (33 shorter events, 0.1 us)
Async XLA Ops:
  2.7 27.7 %slice-start = ((s8[18874368]{0:T(1024)(128)(4,1)}), s8[4194304]{0:T(1024)(128)(4,1)S(1)}, s32[]{:S(2)}) async-start(s8[18874368]{0:T(1024)(128)(4,1)} %bitcast.5), calls=%async_computation.12 | async-start | bytes 8388608
  2.8 27.7 %slice-start.1 = ((s8[18874368]{0:T(1024)(128)(4,1)}), s8[4194304]{0:T(1024)(128)(4,1)S(1)}, s32[]{:S(2)}) async-start(s8[18874368]{0:T(1024)(128)(4,1)} %bitcast.5), calls=%async_computation.13 | async-start | bytes 8388608
  2.8 27.7 %slice-start.2 = ((s8[18874368]{0:T(1024)(128)(4,1)}), s8[4194304]{0:T(1024)(128)(4,1)S(1)}, s32[]{:S(2)}) async-start(s8[18874368]{0:T(1024)(128)(4,1)} %bitcast.5), calls=%async_computation.14 | async-start | bytes 8388608
  2.8 27.7 %slice-start.3 = ((s8[18874368]{0:T(1024)(128)(4,1)}), s8[4194304]{0:T(1024)(128)(4,1)S(1)}, s32[]{:S(2)}) async-start(s8[18874368]{0:T(1024)(128)(4,1)} %bitcast.5), calls=%async_computation.15 | async-start | bytes 8388608
  2.8 27.7 %slice-start.4 = ((s8[18874368]{0:T(1024)(128)(4,1)}), s8[2097152]{0:T(1024)(128)(4,1)S(1)}, s32[]{:S(2)}) async-start(s8[18874368]{0:T(1024)(128)(4,1)} %bitcast.5), calls=%async_computation.16 | async-start | bytes 4194304
  30.5 2.7 %copy-start.3 = (s32[4,384]{1,0:T(4,128)S(1)}, s32[4,384]{1,0:T(4,128)}, u32[]{:S(2)}) copy-start(s32[4,384]{1,0:T(4,128)} %onset_ref.1) | copy-start | bytes 18436
  30.5 2.7 %collective-permute-start = (bf16[64,16,384]{2,1,0:T(8,128)(2,1)S(1)}, bf16[64,16,384]{2,1,0:T(8,128)(2,1)S(1)}, u32[]{:S(2)}, u32[]{:S(2)}) collective-permute-start(bf16[64,16,384]{2,1,0:T(8,128)(2,1)S(1)} %all_to_all.60.x_ref), channel_id=1, source_target_pairs={{0,1},{1,0},{2,3},{3,2},{4,5},{5,4},{6,7},{7,6},{8,9},{9,8},{10,11... | collective-permute-start | bytes 2359304 | tf_op jit(solution)/shard_map/ppermute | solution.py:383
  33.1 16.7 %copy-start = (bf16[544,512]{1,0:T(8,128)(2,1)S(1)}, bf16[544,512]{1,0:T(8,128)(2,1)}, u32[]{:S(2)}) copy-start(bf16[544,512]{1,0:T(8,128)(2,1)} %constant.28.clone.edge_ref) | copy-start | bytes 1671172
  67.1 2.6 %collective-permute-start.1 = (bf16[16,64,384]{2,1,0:T(8,128)(2,1)S(1)}, bf16[16,64,384]{2,1,0:T(8,128)(2,1)S(1)}, u32[]{:S(2)}, u32[]{:S(2)}) collective-permute-start(bf16[16,64,384]{2,1,0:T(8,128)(2,1)S(1)} %all_to_all.62.x_ref), channel_id=1, source_target_pairs={{0,1},{1,0},{2,3},{3,2},{4,5},{5,4},{6,7},{7,6},{8,9},{9,8},{10,11... | collective-permute-start | bytes 2359304 | tf_op jit(solution)/shard_map/ppermute | solution.py:383
  103.7 2.6 %collective-permute-start.2 = (bf16[16,64,384]{2,1,0:T(8,128)(2,1)S(1)}, bf16[16,64,384]{2,1,0:T(8,128)(2,1)S(1)}, u32[]{:S(2)}, u32[]{:S(2)}) collective-permute-start(bf16[16,64,384]{2,1,0:T(8,128)(2,1)S(1)} %all_to_all.64.x_ref), channel_id=1, source_target_pairs={{0,1},{1,0},{2,3},{3,2},{4,5},{5,4},{6,7},{7,6},{8,9},{9,8},{10,11... | collective-permute-start | bytes 2359304 | tf_op jit(solution)/shard_map/ppermute | solution.py:383
  140.2 2.6 %collective-permute-start.3 = (bf16[16,64,384]{2,1,0:T(8,128)(2,1)S(1)}, bf16[16,64,384]{2,1,0:T(8,128)(2,1)S(1)}, u32[]{:S(2)}, u32[]{:S(2)}) collective-permute-start(bf16[16,64,384]{2,1,0:T(8,128)(2,1)S(1)} %all_to_all.66.x_ref), channel_id=1, source_target_pairs={{0,1},{1,0},{2,3},{3,2},{4,5},{5,4},{6,7},{7,6},{8,9},{9,8},{10,11... | collective-permute-start | bytes 2359304 | tf_op jit(solution)/shard_map/ppermute | solution.py:383
  176.8 2.6 %collective-permute-start.4 = (bf16[16,64,384]{2,1,0:T(8,128)(2,1)S(1)}, bf16[16,64,384]{2,1,0:T(8,128)(2,1)S(1)}, u32[]{:S(2)}, u32[]{:S(2)}) collective-permute-start(bf16[16,64,384]{2,1,0:T(8,128)(2,1)S(1)} %all_to_all.68.x_ref), channel_id=1, source_target_pairs={{0,1},{1,0},{2,3},{3,2},{4,5},{5,4},{6,7},{7,6},{8,9},{9,8},{10,11... | collective-permute-start | bytes 2359304 | tf_op jit(solution)/shard_map/ppermute | solution.py:383
  213.4 2.6 %collective-permute-start.5 = (bf16[16,64,384]{2,1,0:T(8,128)(2,1)S(1)}, bf16[16,64,384]{2,1,0:T(8,128)(2,1)S(1)}, u32[]{:S(2)}, u32[]{:S(2)}) collective-permute-start(bf16[16,64,384]{2,1,0:T(8,128)(2,1)S(1)} %all_to_all.70.x_ref), channel_id=1, source_target_pairs={{0,1},{1,0},{2,3},{3,2},{4,5},{5,4},{6,7},{7,6},{8,9},{9,8},{10,11... | collective-permute-start | bytes 2359304 | tf_op jit(solution)/shard_map/ppermute | solution.py:383
  216.0 13.7 %copy-start.1 = (bf16[4,1024,384]{2,1,0:T(8,128)(2,1)S(1)}, bf16[4,1024,384]{2,1,0:T(8,128)(2,1)}, u32[]{:S(2)}) copy-start(bf16[4,1024,384]{2,1,0:T(8,128)(2,1)} %direct_ref.2) | copy-start | bytes 9437188
  216.0 13.7 %copy-start.2 = (bf16[704,128]{1,0:T(8,128)(2,1)S(1)}, bf16[704,128]{1,0:T(8,128)(2,1)}, u32[]{:S(2)}) copy-start(bf16[704,128]{1,0:T(8,128)(2,1)} %constant.32.clone.last_ref) | copy-start | bytes 540676
